TPU v7x, 256 devices: a whole 4x4x8 slice. The times are simulated.
256 devices in a mesh: gx: 32 (over y_hi, z, core), gy: 4 (over x), gz: 2 (over y_lo).
Axes of the slice: x: 4, y: 4 (y_hi: 2, y_lo: 2; y = y_hi * 2 + y_lo), z: 8, core: 2. Of those that a mesh axis runs over, the one named last changes fastest.
Arguments:
- elevation: float32 [2048, 8192], P('gx', ('gy', 'gz')), may hold values from -1 to 1
- surface_potential: float32 [2048, 8192], P('gx', ('gy', 'gz')), may hold values from -2 to 2
- seabed: int32 [2048, 8192], P('gx', 'gy'), may hold values from 384 to 1023
- interior_potential: float32 [16, 2048, 8192], P('gz', 'gx', 'gy'), may hold values from -1.5 to 1.5
Outputs:
- new_elevation: float32 [2048, 8192], P('gx', ('gy', 'gz'))
- new_potential: float32 [2048, 8192], P('gx', ('gy', 'gz'))
- laplace_apply: float32 [16, 2048, 8192], P('gz', 'gx', 'gy')
All inputs are finite; a program needn't handle non-finite values.
Results may differ from a plain program's by a relative error of at most 0.0003.
Values sent between devices are 32-bit elements; how exact they have to be, the bound alone decides.
A program may use at most 64 MiB of HBM per device.

v0:
```python
import jax
import jax.numpy as jnp
from jax import lax
from jax.sharding import PartitionSpec as P

time_step = 0.05
depth_unit = 0.015625


def with_halo(block, sides, width):
    for axis, dim in sides:
        count = lax.axis_size(axis)
        forward = [(i, i + 1) for i in range(count - 1)]
        forward.append((count - 1, 0))
        backward = [(target, source) for source, target in forward]
        low = lax.ppermute(
            lax.slice_in_dim(block, block.shape[dim] - width, None, axis=dim), axis, forward
        )
        high = lax.ppermute(lax.slice_in_dim(block, 0, width, axis=dim), axis, backward)
        block = jnp.concatenate([low, block, high], axis=dim)
    return block


def partner_2(value, axis, bit):
    mask = 2**bit
    pairs = [(source, source ^ mask) for source in range(lax.axis_size(axis))]
    return lax.ppermute(value, axis, pairs)


def window(extended, step_north, step_east, margin):
    height = extended.shape[-2] - 2 * margin
    breadth = extended.shape[-1] - 2 * margin
    return extended[
        ...,
        margin + step_north : margin + step_north + height,
        margin + step_east : margin + step_east + breadth,
    ]


def rates(extended):
    grad_north = (
        8.0 * (window(extended, 1, 0, 2) - window(extended, -1, 0, 2))
        - (window(extended, 2, 0, 2) - window(extended, -2, 0, 2))
    ) / 12.0
    grad_east = (
        8.0 * (window(extended, 0, 1, 2) - window(extended, 0, -1, 2))
        - (window(extended, 0, 2, 2) - window(extended, 0, -2, 2))
    ) / 12.0
    centre = window(extended, 0, 0, 2)
    poten = extended[1]
    curve_north = (
        -window(poten, 2, 0, 2)
        + 16.0 * window(poten, 1, 0, 2)
        - 30.0 * centre[1]
        + 16.0 * window(poten, -1, 0, 2)
        - window(poten, -2, 0, 2)
    )
    curve_east = (
        -window(poten, 0, 2, 2)
        + 16.0 * window(poten, 0, 1, 2)
        - 30.0 * centre[1]
        + 16.0 * window(poten, 0, -1, 2)
        - window(poten, 0, -2, 2)
    )
    curvature = (curve_north + curve_east) / 12.0
    rate_height = curvature - (grad_north[0] * grad_north[1] + grad_east[0] * grad_east[1])
    rate_potential = -centre[0] - 0.5 * (
        grad_north[1] * grad_north[1] + grad_east[1] * grad_east[1]
    )
    return jnp.stack([rate_height, rate_potential])


def shards(elevation, surface_potential, seabed, interior_potential):
    surface_pair = jnp.stack([elevation, surface_potential])
    depth = seabed.astype(jnp.float32) * depth_unit
    layers = interior_potential.shape[0]

    def advance(fields):
        extended = with_halo(fields, (("gx", 1), (("gy", "gz"), 2)), 2)
        return rates(extended)

    section_one = surface_pair + time_step * advance(surface_pair)
    updated = 0.5 * (surface_pair + section_one + time_step * advance(section_one))
    surface = lax.all_gather(updated, "gz", axis=2, tiled=True)
    column = depth + surface[0]
    planes = jnp.stack([column, surface[1], depth])
    volume_wide = with_halo(interior_potential, (("gx", 1), ("gy", 2)), 1)
    plane_wide = with_halo(planes, (("gx", 1), ("gy", 2)), 1)
    layer_group = lax.axis_index("gz")
    bottom_group = layer_group == 0
    outgoing = jnp.where(bottom_group, volume_wide[-1], volume_wide[0])
    partner = partner_2(outgoing, "gz", 0)
    ghost_below = jnp.where(bottom_group, volume_wide[0], partner)
    ghost_above = jnp.where(bottom_group, partner, 2.0 * plane_wide[1] - volume_wide[-1])
    column_stack = jnp.concatenate([ghost_below[None], volume_wide, ghost_above[None]], 0)
    column_centre = plane_wide[0, 1:-1, 1:-1]
    column_north = 0.5 * (plane_wide[0, 2:, 1:-1] - plane_wide[0, :-2, 1:-1])
    column_east = 0.5 * (plane_wide[0, 1:-1, 2:] - plane_wide[0, 1:-1, :-2])
    depth_north = 0.5 * (plane_wide[2, 2:, 1:-1] - plane_wide[2, :-2, 1:-1])
    depth_east = 0.5 * (plane_wide[2, 1:-1, 2:] - plane_wide[2, 1:-1, :-2])
    total_layers = layers * lax.axis_size("gz")
    sigma_level = (
        (layer_group * layers + jnp.arange(layers, dtype=jnp.int32)).astype(jnp.float32) + 0.5
    ) / total_layers
    sigma_level = sigma_level[:, None, None]
    slope_north = (depth_north - sigma_level * column_north) / column_centre
    slope_east = (depth_east - sigma_level * column_east) / column_centre
    spacing = 1.0 / total_layers
    middle_stack = column_stack[1:-1]
    upper_stack = column_stack[2:]
    lower_stack = column_stack[:-2]
    centre = middle_stack[:, 1:-1, 1:-1]
    second_north = middle_stack[:, 2:, 1:-1] - 2.0 * centre + middle_stack[:, :-2, 1:-1]
    second_east = middle_stack[:, 1:-1, 2:] - 2.0 * centre + middle_stack[:, 1:-1, :-2]
    mixed_north = (
        upper_stack[:, 2:, 1:-1]
        - upper_stack[:, :-2, 1:-1]
        - lower_stack[:, 2:, 1:-1]
        + lower_stack[:, :-2, 1:-1]
    ) / (4.0 * spacing)
    mixed_east = (
        upper_stack[:, 1:-1, 2:]
        - upper_stack[:, 1:-1, :-2]
        - lower_stack[:, 1:-1, 2:]
        + lower_stack[:, 1:-1, :-2]
    ) / (4.0 * spacing)
    vertical = (upper_stack[:, 1:-1, 1:-1] - 2.0 * centre + lower_stack[:, 1:-1, 1:-1]) / (
        spacing * spacing
    )
    weight = (
        slope_north * slope_north + slope_east * slope_east + 1.0 / (column_centre * column_centre)
    )
    laplace_apply = (
        second_north
        + second_east
        + 2.0 * slope_north * mixed_north
        + 2.0 * slope_east * mixed_east
        + weight * vertical
    )
    return (updated[0], updated[1], laplace_apply)


def solution(mesh):
    return jax.shard_map(
        shards,
        mesh=mesh,
        in_specs=(P("gx", ("gy", "gz")), P("gx", ("gy", "gz")), P("gx", "gy"), P("gz", "gx", "gy")),
        out_specs=(P("gx", ("gy", "gz")), P("gx", ("gy", "gz")), P("gz", "gx", "gy")),
        check_vma=False,
    )
```

profile of v0, /device:TPU:6, one launch (start us, length us, event | category | flops | bytes accessed | tf_op | source)
XLA Modules:
  0.0 146.0 jit_solution(1554330425581716681)
XLA Ops:
  7.2 0.9 fusion.92
  8.1 8.0 %collective-permute-start.1 = (f32[2,2,1024]{2,1,0:T(2,128)S(1)}, f32[2,2,1024]{2,1,0:T(2,128)S(1)}, u32[]{:S(2)}, u32[]{:S(2)}) collective-permute-start(f32[2,2,1024]{2,1,0:T(2,128)S(1)} %get-tuple-element.35), channel_id=1, source_target_pairs={{8,0},{16,8},{24,16},{32,24},{40,32},{48,40},{56,48},{64,56},{72,6... | collective-permute-start | bytes 49160 | tf_op jit(solution)/shard_map/ppermute | solution.py:19
  16.1 1.4 collective-permute-done.1
  17.6 5.3 %collective-permute-done = f32[2,2,1024]{2,1,0:T(2,128)S(1)} collective-permute-done((f32[2,2,1024]{2,1,0:T(2,128)S(1)}, f32[2,2,1024]{2,1,0:T(2,128)S(1)}, u32[]{:S(2)}, u32[]{:S(2)}) %collective-permute-start) | collective-permute-done | bytes 16416 | tf_op jit(solution)/shard_map/ppermute | solution.py:16
  22.9 1.1 pad_maximum_fusion.15
  24.0 0.1 fusion.99
  24.1 1.0 collective-permute-start.3
  25.1 1.1 collective-permute-start.2
  26.2 1.3 pad_maximum_fusion.16
  27.5 0.2 fusion.59
  27.7 0.8 collective-permute-done.3
  28.5 1.8 %collective-permute-done.2 = f32[2,68,2]{2,1,0:T(8,128)S(1)} collective-permute-done((f32[2,68,2]{2,1,0:T(8,128)S(1)}, f32[2,68,2]{2,1,0:T(8,128)S(1)}, u32[]{:S(2)}, u32[]{:S(2)}) %collective-permute-start.2) | collective-permute-done | bytes 1120 | tf_op jit(solution)/shard_map/ppermute | solution.py:16
  30.4 0.4 concatenate.92
  30.8 0.3 pad_maximum_fusion.13
  31.1 0.5 fusion.56
  31.5 0.6 fusion.82
  32.1 0.1 fusion.61
  32.2 0.1 collective-permute-start.5
  32.3 0.5 collective-permute-start.4
  32.8 0.9 collective-permute-done.5
  33.7 5.5 %collective-permute-done.4 = f32[2,2,1024]{2,1,0:T(2,128)S(1)} collective-permute-done((f32[2,2,1024]{2,1,0:T(2,128)S(1)}, f32[2,2,1024]{2,1,0:T(2,128)S(1)}, u32[]{:S(2)}, u32[]{:S(2)}) %collective-permute-start.4) | collective-permute-done | bytes 16416 | tf_op jit(solution)/shard_map/ppermute | solution.py:16
  39.3 0.1 pad_maximum_fusion.17
  39.3 0.1 fusion.98
  39.4 0.8 collective-permute-start.7
  40.2 1.3 collective-permute-start.6
  41.5 0.3 fusion.38
  41.8 2.1 %collective-permute-done.7 = f32[2,68,2]{2,1,0:T(8,128)S(1)} collective-permute-done((f32[2,68,2]{2,1,0:T(8,128)S(1)}, f32[2,68,2]{2,1,0:T(8,128)S(1)}, u32[]{:S(2)}, u32[]{:S(2)}) %collective-permute-start.7) | collective-permute-done | bytes 1120 | tf_op jit(solution)/shard_map/ppermute | solution.py:19
  43.9 1.6 %collective-permute-done.6 = f32[2,68,2]{2,1,0:T(8,128)S(1)} collective-permute-done((f32[2,68,2]{2,1,0:T(8,128)S(1)}, f32[2,68,2]{2,1,0:T(8,128)S(1)}, u32[]{:S(2)}, u32[]{:S(2)}) %collective-permute-start.6) | collective-permute-done | bytes 1120 | tf_op jit(solution)/shard_map/ppermute | solution.py:16
  45.5 0.4 concatenate.98
  45.9 0.3 pad_maximum_fusion.14
  46.2 0.5 fusion.52
  46.6 0.1 fusion.65
  46.7 0.5 fusion.69
  47.3 0.9 fusion.63
  48.2 1.3 fusion.96
  49.5 0.1 collective-permute-start.8
  49.6 0.5 collective-permute-start.9
  50.1 1.4 collective-permute-done.8
  51.5 5.7 %collective-permute-done.9 = f32[8,1,2048]{2,1,0:T(1,128)S(1)} collective-permute-done((f32[8,1,2048]{2,1,0:T(1,128)S(1)}, f32[8,1,2048]{2,1,0:T(1,128)S(1)}, u32[]{:S(2)}, u32[]{:S(2)}) %collective-permute-start.9) | collective-permute-done | bytes 65568 | tf_op jit(solution)/shard_map/ppermute | solution.py:16
  57.2 5.6 %pad_maximum_fusion = f32[8,66,2048]{2,1,0:T(8,128)} fusion(f32[8,1,2048]{2,1,0:T(1,128)S(1)} %collective-permute-done.8, f32[8,64,2048]{2,1,0:T(8,128)} %param.7, f32[8,1,2048]{2,1,0:T(1,128)S(1)} %collective-permute-done.9), kind=kLoop, calls=%fused_computation.16 | loop fusion | flops 2162688 | bytes 8650752 | tf_op jit(solution)/shard_map/concatenate | solution.py:20
  62.8 1.2 fusion.95
  64.0 4.1 %collective-permute-start.11 = (f32[8,66,1]{2,1,0:T(8,128)S(1)}, f32[8,66,1]{2,1,0:T(8,128)S(1)}, u32[]{:S(2)}, u32[]{:S(2)}) collective-permute-start(f32[8,66,1]{2,1,0:T(8,128)S(1)} %get-tuple-element.8), channel_id=1, source_target_pairs={{0,2},{2,4},{4,6},{6,0},{1,3},{3,5},{5,7},{7,1},{8,10},{10,12},{12... | collective-permute-start | bytes 6344 | tf_op jit(solution)/shard_map/ppermute | solution.py:16
  68.1 0.8 slice_bitcast_fusion.5
  68.9 3.4 %collective-permute-done.11 = f32[8,66,1]{2,1,0:T(8,128)S(1)} collective-permute-done((f32[8,66,1]{2,1,0:T(8,128)S(1)}, f32[8,66,1]{2,1,0:T(8,128)S(1)}, u32[]{:S(2)}, u32[]{:S(2)}) %collective-permute-start.11) | collective-permute-done | bytes 2144 | tf_op jit(solution)/shard_map/ppermute | solution.py:16
  72.3 3.7 %collective-permute-done.10 = f32[8,66,1]{2,1,0:T(8,128)S(1)} collective-permute-done((f32[8,66,1]{2,1,0:T(8,128)S(1)}, f32[8,66,1]{2,1,0:T(8,128)S(1)}, u32[]{:S(2)}, u32[]{:S(2)}) %collective-permute-start.10) | collective-permute-done | bytes 2144 | tf_op jit(solution)/shard_map/ppermute | solution.py:19
  76.0 6.8 %concatenate.110 = f32[8,66,2050]{2,1,0:T(8,128)} concatenate(f32[8,66,1]{2,1,0:T(8,128)S(1)} %collective-permute-done.11, f32[8,66,2048]{2,1,0:T(8,128)} %pad_maximum_fusion, f32[8,66,1]{2,1,0:T(8,128)S(1)} %collective-permute-done.10), dimensions={2} | concatenate | bytes 8659200 | tf_op jit(solution)/shard_map/concatenate | solution.py:20
  82.9 1.1 slice.468
  84.0 1.2 multiply_divide_fusion
  85.2 0.1 collective-permute-start.12
  85.3 0.5 collective-permute-start.13
  85.8 2.2 %fusion.33 = f32[66,2050]{1,0:T(8,128)} fusion(f32[8,66,2050]{2,1,0:T(8,128)} %concatenate.110, pred[]{:T(512)S(6)} %eq.3), kind=kLoop, calls=%fused_computation.83 | loop fusion | flops 135300 | bytes 1623601 | tf_op jit(solution)/shard_map/jit(_where)/select_n | solution.py:91
  87.9 4.4 %collective-permute-done.13 = f32[3,1,2048]{2,1,0:T(1,128)S(1)} collective-permute-done((f32[3,1,2048]{2,1,0:T(1,128)S(1)}, f32[3,1,2048]{2,1,0:T(1,128)S(1)}, u32[]{:S(2)}, u32[]{:S(2)}) %collective-permute-start.13) | collective-permute-done | bytes 24608 | tf_op jit(solution)/shard_map/ppermute | solution.py:16
  92.3 1.5 pad_maximum_fusion.11
  93.8 1.0 fusion.97
  94.8 0.2 collective-permute-start.15
  95.0 1.9 %collective-permute-start.16 = (f32[3,66,1]{2,1,0:T(8,128)S(1)}, f32[3,66,1]{2,1,0:T(8,128)}, u32[]{:S(2)}, u32[]{:S(2)}) collective-permute-start(f32[3,66,1]{2,1,0:T(8,128)S(1)} %get-tuple-element.11), channel_id=1, source_target_pairs={{2,0},{4,2},{6,4},{0,6},{3,1},{5,3},{7,5},{1,7},{10,8},{12,10},{14... | collective-permute-start | bytes 2384 | tf_op jit(solution)/shard_map/ppermute | solution.py:19
  96.9 1.1 fusion.49
  98.0 1.6 %collective-permute-done.15 = f32[3,66,1]{2,1,0:T(8,128)S(1)} collective-permute-done((f32[3,66,1]{2,1,0:T(8,128)S(1)}, f32[3,66,1]{2,1,0:T(8,128)S(1)}, u32[]{:S(2)}, u32[]{:S(2)}) %collective-permute-start.15) | collective-permute-done | bytes 824 | tf_op jit(solution)/shard_map/ppermute | solution.py:16
  99.7 1.4 collective-permute-done.16
  101.1 2.9 %concatenate.112 = f32[3,66,2050]{2,1,0:T(8,128)} concatenate(f32[3,66,1]{2,1,0:T(8,128)S(1)} %collective-permute-done.15, f32[3,66,2048]{2,1,0:T(8,128)} %pad_maximum_fusion.11, f32[3,66,1]{2,1,0:T(8,128)} %collective-permute-done.16), dimensions={2} | concatenate | bytes 3247200 | tf_op jit(solution)/shard_map/concatenate | solution.py:20
  104.0 2.1 %fusion.42 = f32[64,2048]{1,0:T(8,128)} fusion(f32[3,66,1]{2,1,0:T(8,128)S(1)} %collective-permute-done.15, f32[3,1,2048]{2,1,0:T(1,128)} %copy-done.8, f32[3,1,2048]{2,1,0:T(1,128)} %copy-done.9, f32[1,64,2048]{2,1,0:T(8,128)S(1)} %get-tuple-element.27, f32[1,64,2048]{2,1,0:T(8,128)S(1)} %slice.468, f32[1,64,2048]{2,1,0:T(8,128)S(1)} %bitcast.81, ...), kind=kLoop, calls=%fused_computation.93 | loop fusion | flops 1572864 | bytes 2147888 | tf_op jit(solution)/shard_map/mul | solution.py:107
  106.1 2.0 %fusion.44 = f32[64,2048]{1,0:T(8,128)} fusion(f32[3,66,1]{2,1,0:T(8,128)S(1)} %collective-permute-done.15, f32[3,1,2048]{2,1,0:T(1,128)} %copy-done.8, f32[3,1,2048]{2,1,0:T(1,128)} %copy-done.9, f32[1,64,2048]{2,1,0:T(8,128)S(1)} %get-tuple-element.27, f32[1,64,2048]{2,1,0:T(8,128)S(1)} %slice.468, f32[1,64,2048]{2,1,0:T(8,128)S(1)} %bitcast.82, ...), kind=kLoop, calls=%fused_computation.105 | loop fusion | flops 1572864 | bytes 2147888 | tf_op jit(solution)/shard_map/sub | solution.py:107
  108.1 1.8 %fusion.32 = (f32[1,66,2050]{2,1,0:T(8,128)S(1)}, f32[1,66,2050]{2,1,0:T(8,128)S(1)}) fusion(f32[66,2050]{1,0:T(8,128)} %collective-permute-done.14, f32[3,66,2050]{2,1,0:T(8,128)} %concatenate.112, f32[8,66,2050]{2,1,0:T(8,128)} %concatenate.110, pred[]{:T(512)S(6)} %eq.3), kind=kLoop, calls=%fused_computation.71 | loop fusion | flops 541200 | bytes 3247201 | tf_op jit(solution)/shard_map/broadcast_in_dim | solution.py:95
  109.9 29.2 %fusion.5 = f32[8,64,2048]{2,1,0:T(8,128)} fusion(f32[8,66,2050]{2,1,0:T(8,128)S(1)} %bitcast.77, f32[1,66,2050]{2,1,0:T(8,128)S(1)} %get-tuple-element.6, f32[1,66,2050]{2,1,0:T(8,128)S(1)} %get-tuple-element.5, f32[8,66,1]{2,1,0:T(8,128)S(1)} %copy-done.5, f32[8,1,2048]{2,1,0:T(1,128)S(1)} %copy-done.11, f32[8,64,2048]{2,1,0:T(8,128)} %param.7, ...), kind=kLoop, calls=%fused_computation.22 | loop fusion | flops 55574528 | bytes 17081664 | tf_op jit(solution)/shard_map/add | solution.py:134
  (44 shorter events, 0.2 us)
Async XLA Ops:
  7.2 75.7 %all-gather.2.cloned.1.call-start = ((), (), s32[]{:S(2)}) async-start(), calls=%async_computation | async-start | bytes 1572864 | tf_op jit(solution)/shard_map/all_gather | solution.py:84
  7.2 23.5 %copy-start = (f32[64,1024]{1,0:T(8,128)S(1)}, f32[64,1024]{1,0:T(8,128)}, u32[]{:S(2)}) copy-start(f32[64,1024]{1,0:T(8,128)} %param.4) | copy-start | bytes 786436
  7.2 23.5 %copy-start.1 = (f32[64,1024]{1,0:T(8,128)S(1)}, f32[64,1024]{1,0:T(8,128)}, u32[]{:S(2)}) copy-start(f32[64,1024]{1,0:T(8,128)} %param.5) | copy-start | bytes 786436
  8.1 9.4 %collective-permute-start.1 = (f32[2,2,1024]{2,1,0:T(2,128)S(1)}, f32[2,2,1024]{2,1,0:T(2,128)S(1)}, u32[]{:S(2)}, u32[]{:S(2)}) collective-permute-start(f32[2,2,1024]{2,1,0:T(2,128)S(1)} %get-tuple-element.35), channel_id=1, source_target_pairs={{8,0},{16,8},{24,16},{32,24},{40,32},{48,40},{56,48},{64,56},{72,6... | collective-permute-start | bytes 49160 | tf_op jit(solution)/shard_map/ppermute | solution.py:19
  16.1 6.8 %collective-permute-start = (f32[2,2,1024]{2,1,0:T(2,128)S(1)}, f32[2,2,1024]{2,1,0:T(2,128)S(1)}, u32[]{:S(2)}, u32[]{:S(2)}) collective-permute-start(f32[2,2,1024]{2,1,0:T(2,128)S(1)} %get-tuple-element.34), channel_id=1, source_target_pairs={{0,8},{8,16},{16,24},{24,32},{32,40},{40,48},{48,56},{56,64},{64,7... | collective-permute-start | bytes 49160 | tf_op jit(solution)/shard_map/ppermute | solution.py:16
  24.1 4.4 %collective-permute-start.3 = (f32[2,68,2]{2,1,0:T(8,128)S(1)}, f32[2,68,2]{2,1,0:T(8,128)S(1)}, u32[]{:S(2)}, u32[]{:S(2)}) collective-permute-start(f32[2,68,2]{2,1,0:T(8,128)S(1)} %get-tuple-element.21), channel_id=1, source_target_pairs={{1,0},{2,1},{3,2},{4,3},{5,4},{6,5},{7,6},{0,7},{9,8},{10,9},{11,1... | collective-permute-start | bytes 3272 | tf_op jit(solution)/shard_map/ppermute | solution.py:19
  25.1 5.3 %collective-permute-start.2 = (f32[2,68,2]{2,1,0:T(8,128)S(1)}, f32[2,68,2]{2,1,0:T(8,128)S(1)}, u32[]{:S(2)}, u32[]{:S(2)}) collective-permute-start(f32[2,68,2]{2,1,0:T(8,128)S(1)} %get-tuple-element.22), channel_id=1, source_target_pairs={{0,1},{1,2},{2,3},{3,4},{4,5},{5,6},{6,7},{7,0},{8,9},{9,10},{10,1... | collective-permute-start | bytes 3272 | tf_op jit(solution)/shard_map/ppermute | solution.py:16
  32.2 1.5 %collective-permute-start.5 = (f32[2,2,1024]{2,1,0:T(2,128)S(1)}, f32[2,2,1024]{2,1,0:T(2,128)S(1)}, u32[]{:S(2)}, u32[]{:S(2)}) collective-permute-start(f32[2,2,1024]{2,1,0:T(2,128)S(1)} %get-tuple-element.31), channel_id=1, source_target_pairs={{8,0},{16,8},{24,16},{32,24},{40,32},{48,40},{56,48},{64,56},{72,6... | collective-permute-start | bytes 49160 | tf_op jit(solution)/shard_map/ppermute | solution.py:19
  32.3 7.0 %collective-permute-start.4 = (f32[2,2,1024]{2,1,0:T(2,128)S(1)}, f32[2,2,1024]{2,1,0:T(2,128)S(1)}, u32[]{:S(2)}, u32[]{:S(2)}) collective-permute-start(f32[2,2,1024]{2,1,0:T(2,128)S(1)} %get-tuple-element.30), channel_id=1, source_target_pairs={{0,8},{8,16},{16,24},{24,32},{32,40},{40,48},{48,56},{56,64},{64,7... | collective-permute-start | bytes 49160 | tf_op jit(solution)/shard_map/ppermute | solution.py:16
  39.4 4.4 %collective-permute-start.7 = (f32[2,68,2]{2,1,0:T(8,128)S(1)}, f32[2,68,2]{2,1,0:T(8,128)S(1)}, u32[]{:S(2)}, u32[]{:S(2)}) collective-permute-start(f32[2,68,2]{2,1,0:T(8,128)S(1)} %get-tuple-element.19), channel_id=1, source_target_pairs={{1,0},{2,1},{3,2},{4,3},{5,4},{6,5},{7,6},{0,7},{9,8},{10,9},{11,1... | collective-permute-start | bytes 3272 | tf_op jit(solution)/shard_map/ppermute | solution.py:19
  40.2 5.3 %collective-permute-start.6 = (f32[2,68,2]{2,1,0:T(8,128)S(1)}, f32[2,68,2]{2,1,0:T(8,128)S(1)}, u32[]{:S(2)}, u32[]{:S(2)}) collective-permute-start(f32[2,68,2]{2,1,0:T(8,128)S(1)} %get-tuple-element.20), channel_id=1, source_target_pairs={{0,1},{1,2},{2,3},{3,4},{4,5},{5,6},{6,7},{7,0},{8,9},{9,10},{10,1... | collective-permute-start | bytes 3272 | tf_op jit(solution)/shard_map/ppermute | solution.py:16
  49.5 2.0 %collective-permute-start.8 = (f32[8,1,2048]{2,1,0:T(1,128)S(1)}, f32[8,1,2048]{2,1,0:T(1,128)S(1)}, u32[]{:S(2)}, u32[]{:S(2)}) collective-permute-start(f32[8,1,2048]{2,1,0:T(1,128)S(1)} %get-tuple-element.10), channel_id=1, source_target_pairs={{8,0},{16,8},{24,16},{32,24},{40,32},{48,40},{56,48},{64,56},{72,6... | collective-permute-start | bytes 196616 | tf_op jit(solution)/shard_map/ppermute | solution.py:19
  49.6 7.6 %collective-permute-start.9 = (f32[8,1,2048]{2,1,0:T(1,128)S(1)}, f32[8,1,2048]{2,1,0:T(1,128)S(1)}, u32[]{:S(2)}, u32[]{:S(2)}) collective-permute-start(f32[8,1,2048]{2,1,0:T(1,128)S(1)} %get-tuple-element.9), channel_id=1, source_target_pairs={{0,8},{8,16},{16,24},{24,32},{32,40},{40,48},{48,56},{56,64},{64,7... | collective-permute-start | bytes 196616 | tf_op jit(solution)/shard_map/ppermute | solution.py:16
  50.1 18.0 %copy-start.2 = (f32[2,64,1024]{2,1,0:T(8,128)S(1)}, f32[2,64,1024]{2,1,0:T(8,128)}, u32[]{:S(2)}) copy-start(f32[2,64,1024]{2,1,0:T(8,128)} %fusion.63) | copy-start | bytes 1572868
  51.5 11.2 %copy-start.10 = (f32[8,1,2048]{2,1,0:T(1,128)}, f32[8,1,2048]{2,1,0:T(1,128)S(1)}, u32[]{:S(2)}) copy-start(f32[8,1,2048]{2,1,0:T(1,128)S(1)} %collective-permute-done.8) | copy-start | bytes 196612
  57.2 5.6 %copy-start.12 = (f32[8,1,2048]{2,1,0:T(1,128)}, f32[8,1,2048]{2,1,0:T(1,128)S(1)}, u32[]{:S(2)}) copy-start(f32[8,1,2048]{2,1,0:T(1,128)S(1)} %collective-permute-done.9) | copy-start | bytes 196612
  64.0 8.4 %collective-permute-start.11 = (f32[8,66,1]{2,1,0:T(8,128)S(1)}, f32[8,66,1]{2,1,0:T(8,128)S(1)}, u32[]{:S(2)}, u32[]{:S(2)}) collective-permute-start(f32[8,66,1]{2,1,0:T(8,128)S(1)} %get-tuple-element.8), channel_id=1, source_target_pairs={{0,2},{2,4},{4,6},{6,0},{1,3},{3,5},{5,7},{7,1},{8,10},{10,12},{12... | collective-permute-start | bytes 6344 | tf_op jit(solution)/shard_map/ppermute | solution.py:16
  68.1 7.9 %collective-permute-start.10 = (f32[8,66,1]{2,1,0:T(8,128)S(1)}, f32[8,66,1]{2,1,0:T(8,128)S(1)}, u32[]{:S(2)}, u32[]{:S(2)}) collective-permute-start(f32[8,66,1]{2,1,0:T(8,128)S(1)} %get-tuple-element.7), channel_id=1, source_target_pairs={{2,0},{4,2},{6,4},{0,6},{3,1},{5,3},{7,5},{1,7},{10,8},{12,10},{14... | collective-permute-start | bytes 6344 | tf_op jit(solution)/shard_map/ppermute | solution.py:19
  68.9 15.0 %copy-start.7 = (s32[64,2048]{1,0:T(8,128)S(1)}, s32[64,2048]{1,0:T(8,128)}, u32[]{:S(2)}) copy-start(s32[64,2048]{1,0:T(8,128)} %param.6) | copy-start | bytes 1572868
  72.3 10.5 %copy-start.4 = (f32[8,66,1]{2,1,0:T(8,128)}, f32[8,66,1]{2,1,0:T(8,128)S(1)}, u32[]{:S(2)}) copy-start(f32[8,66,1]{2,1,0:T(8,128)S(1)} %collective-permute-done.11) | copy-start | bytes 6340
  76.0 6.8 %copy-start.6 = (f32[8,66,1]{2,1,0:T(8,128)}, f32[8,66,1]{2,1,0:T(8,128)S(1)}, u32[]{:S(2)}) copy-start(f32[8,66,1]{2,1,0:T(8,128)S(1)} %collective-permute-done.10) | copy-start | bytes 6340
  85.2 2.8 %collective-permute-start.12 = (f32[3,1,2048]{2,1,0:T(1,128)S(1)}, f32[3,1,2048]{2,1,0:T(1,128)S(1)}, u32[]{:S(2)}, u32[]{:S(2)}) collective-permute-start(f32[3,1,2048]{2,1,0:T(1,128)S(1)} %get-tuple-element.16), channel_id=1, source_target_pairs={{8,0},{16,8},{24,16},{32,24},{40,32},{48,40},{56,48},{64,56},{72,6... | collective-permute-start | bytes 73736 | tf_op jit(solution)/shard_map/ppermute | solution.py:19
  85.3 7.0 %collective-permute-start.13 = (f32[3,1,2048]{2,1,0:T(1,128)S(1)}, f32[3,1,2048]{2,1,0:T(1,128)S(1)}, u32[]{:S(2)}, u32[]{:S(2)}) collective-permute-start(f32[3,1,2048]{2,1,0:T(1,128)S(1)} %get-tuple-element.15), channel_id=1, source_target_pairs={{0,8},{8,16},{16,24},{24,32},{32,40},{40,48},{48,56},{56,64},{64,7... | collective-permute-start | bytes 73736 | tf_op jit(solution)/shard_map/ppermute | solution.py:16
  87.9 20.2 %collective-permute-start.14 = (f32[66,2050]{1,0:T(8,128)}, f32[66,2050]{1,0:T(8,128)}, u32[]{:S(2)}, u32[]{:S(2)}) collective-permute-start(f32[66,2050]{1,0:T(8,128)} %fusion.33), channel_id=1, source_target_pairs={{0,1},{1,0},{2,3},{3,2},{4,5},{5,4},{6,7},{7,6},{8,9},{9,8},{10,11... | collective-permute-start | bytes 1623608 | tf_op jit(solution)/shard_map/ppermute | solution.py:27
  87.9 11.7 %copy-start.8 = (f32[3,1,2048]{2,1,0:T(1,128)}, f32[3,1,2048]{2,1,0:T(1,128)S(1)}, u32[]{:S(2)}) copy-start(f32[3,1,2048]{2,1,0:T(1,128)S(1)} %collective-permute-done.12) | copy-start | bytes 73732
  92.3 7.3 %copy-start.9 = (f32[3,1,2048]{2,1,0:T(1,128)}, f32[3,1,2048]{2,1,0:T(1,128)S(1)}, u32[]{:S(2)}) copy-start(f32[3,1,2048]{2,1,0:T(1,128)S(1)} %collective-permute-done.13) | copy-start | bytes 73732
  94.8 4.8 %collective-permute-start.15 = (f32[3,66,1]{2,1,0:T(8,128)S(1)}, f32[3,66,1]{2,1,0:T(8,128)S(1)}, u32[]{:S(2)}, u32[]{:S(2)}) collective-permute-start(f32[3,66,1]{2,1,0:T(8,128)S(1)} %get-tuple-element.12), channel_id=1, source_target_pairs={{0,2},{2,4},{4,6},{6,0},{1,3},{3,5},{5,7},{7,1},{8,10},{10,12},{12... | collective-permute-start | bytes 2384 | tf_op jit(solution)/shard_map/ppermute | solution.py:16
  95.0 6.1 %collective-permute-start.16 = (f32[3,66,1]{2,1,0:T(8,128)S(1)}, f32[3,66,1]{2,1,0:T(8,128)}, u32[]{:S(2)}, u32[]{:S(2)}) collective-permute-start(f32[3,66,1]{2,1,0:T(8,128)S(1)} %get-tuple-element.11), channel_id=1, source_target_pairs={{2,0},{4,2},{6,4},{0,6},{3,1},{5,3},{7,5},{1,7},{10,8},{12,10},{14... | collective-permute-start | bytes 2384 | tf_op jit(solution)/shard_map/ppermute | solution.py:19
  101.1 8.8 %slice-start = ((s8[5013504]{0:T(1024)(128)(4,1)}), s8[819200]{0:T(1024)(128)(4,1)S(1)}, s32[]{:S(2)}) async-start(s8[5013504]{0:T(1024)(128)(4,1)} %bitcast.76), calls=%async_computation.1 | async-start | bytes 1638400
  103.9 5.9 %slice-start.1 = ((s8[5013504]{0:T(1024)(128)(4,1)}), s8[4194304]{0:T(1024)(128)(4,1)S(1)}, s32[]{:S(2)}) async-start(s8[5013504]{0:T(1024)(128)(4,1)} %bitcast.76), calls=%async_computation.2 | async-start | bytes 8388608
  103.9 6.0 %copy-start.3 = (f32[64,2048]{1,0:T(8,128)S(1)}, f32[64,2048]{1,0:T(8,128)}, u32[]{:S(2)}) copy-start(f32[64,2048]{1,0:T(8,128)} %get-tuple-element.14) | copy-start | bytes 1572868
  103.9 6.0 %copy-start.5 = (f32[8,66,1]{2,1,0:T(8,128)S(1)}, f32[8,66,1]{2,1,0:T(8,128)}, u32[]{:S(2)}) copy-start(f32[8,66,1]{2,1,0:T(8,128)} %copy-done.4) | copy-start | bytes 6340
  104.0 6.0 %copy-start.11 = (f32[8,1,2048]{2,1,0:T(1,128)S(1)}, f32[8,1,2048]{2,1,0:T(1,128)}, u32[]{:S(2)}) copy-start(f32[8,1,2048]{2,1,0:T(1,128)} %copy-done.10) | copy-start | bytes 196612
Sparse Core Ops, SparseCore 0:
  48.3 22.4 all-gather.1
where the time goes:
time: 147 us; the launch traced here: 146 us
  other arithmetic  54.2 us (37%)
  waiting for transfers between devices  41.2 us (28%)
  starting transfers between devices  20.2 us (14%)
  local copies, waits for them, and re-layouts  16.1 us (11%)
  between operations  14.4 us (10%)
    ppermute x8, waiting for transfers between devices, with_halo(): lax.ppermute(lax.slice_in_dim(block, block.shape[dim] - width, None, axis...  29.4 us
    add x1, other arithmetic, shards(): second_north + second_east + 2.0 * slope_north * mixed_north  29.2 us
    ppermute x8, starting transfers between devices, with_halo(): lax.ppermute(lax.slice_in_dim(block, 0, width, axis=dim), axis, backward)  12 us
    ppermute x8, waiting for transfers between devices, with_halo(): lax.ppermute(lax.slice_in_dim(block, 0, width, axis=dim), axis, backward)  11.8 us
    concatenate x4, local copies, waits for them, and re-layouts, with_halo(): block = jnp.concatenate([low, block, high], axis=dim)  10.4 us
    concatenate x7, other arithmetic, with_halo(): block = jnp.concatenate([low, block, high], axis=dim)  10.1 us
    ppermute x8, starting transfers between devices, with_halo(): lax.ppermute(lax.slice_in_dim(block, block.shape[dim] - width, None, axis...  8.19 us
  transfers between devices with their start and end apart: 18, of which 15 were waited for; matrix products, arithmetic and copies ran while one was open for 21% of the time, Pallas kernels for 0%

commit v1 on v0

v1 whole, which is shorter than its diff:
```python
import jax
import jax.numpy as jnp
from jax import lax
from jax.experimental import pallas as pl
from jax.experimental.pallas import tpu as pltpu
from jax.sharding import PartitionSpec as P

MESH = pl.DeviceIdType.MESH
TIME_STEP = 0.05
DEPTH_UNIT = 0.015625

ROWS = 64
HALF = 1024
WIDE = 2048
LAYERS = 8
STRIP = 256


def lane_shift(x, by):
    return pltpu.roll(x, (-by) % x.shape[-1], axis=len(x.shape) - 1)


def row_shift(before, here, after, by):
    rows = lax.broadcasted_iota(jnp.int32, here.shape, 0)
    moved = pltpu.roll(here, (-by) % 8, axis=0)
    if by > 0:
        return jnp.where(rows >= 8 - by, pltpu.roll(after, 8 - by, axis=0), moved)
    return jnp.where(rows < -by, pltpu.roll(before, -by, axis=0), moved)


def section(height, poten):
    def parts(tiles):
        before, here, after = tiles
        north = [row_shift(before, here, after, by) for by in (-2, -1, 1, 2)]
        east = [lane_shift(here, by) for by in (-2, -1, 1, 2)]
        return north, east

    def first(m2, m1, p1, p2):
        return 8.0 * (p1 - m1) - (p2 - m2)

    height_north, height_east = parts(height)
    poten_north, poten_east = parts(poten)
    e_n, e_e = first(*height_north), first(*height_east)
    p_n, p_e = first(*poten_north), first(*poten_east)
    near = (poten_north[1] + poten_north[2]) + (poten_east[1] + poten_east[2])
    far = (poten_north[0] + poten_north[3]) + (poten_east[0] + poten_east[3])
    curve = 16.0 * near - far - 60.0 * poten[1]
    rate_height = curve * (1.0 / 12.0) - (e_n * p_n + e_e * p_e) * (1.0 / 144.0)
    rate_poten = -height[1] - (p_n * p_n + p_e * p_e) * (0.5 / 144.0)
    return rate_height, rate_poten


def kernel(
    e_hbm, p_hbm, seabed_hbm, vol_hbm,
    new_e_out, new_p_out, lap_ref,
    raw, one, new, seabed, vol, depth, column,
    local_sem, send_sem, recv_sem,
):
    gx, gy, gz = lax.axis_index("gx"), lax.axis_index("gy"), lax.axis_index("gz")
    block = 2 * gy + gz

    def device(dx, db):
        at = lax.rem(block + db + 8, 8)
        return (lax.rem(gx + dx + 32, 32), lax.div(at, 2), lax.rem(at, 2))

    side = 1 - 2 * gz
    partner = (gx, gy, 1 - gz)
    ghost = 9 * gz
    edge = 7 * (1 - gz)
    own = pl.multiple_of(128 + HALF * gz, 128)
    outer = pl.multiple_of((WIDE + 128) * gz, 128)

    mid = pl.ds(8, ROWS)
    loads = [
        pltpu.make_async_copy(e_hbm, raw.at[0, mid, pl.ds(128, HALF)], local_sem.at[0]),
        pltpu.make_async_copy(p_hbm, raw.at[1, mid, pl.ds(128, HALF)], local_sem.at[1]),
        pltpu.make_async_copy(seabed_hbm, seabed.at[mid, pl.ds(128, WIDE)], local_sem.at[2]),
        pltpu.make_async_copy(
            vol_hbm, vol.at[pl.ds(1, LAYERS), mid, pl.ds(128, WIDE)], local_sem.at[3]
        ),
    ]
    for load in loads:
        load.start()

    near = [(dx, db) for dx in (-1, 0, 1) for db in (-1, 0, 1) if (dx, db) != (0, 0)]
    barrier = pltpu.get_barrier_semaphore()
    for dx, db in near + [(0, -2), (0, 2)]:
        pl.semaphore_signal(barrier, inc=1, device_id=device(dx, db), device_id_type=MESH)
    pl.semaphore_signal(barrier, inc=1, device_id=device(0, 3 * side), device_id_type=MESH)
    pl.semaphore_wait(barrier, 11)

    copies = []

    def send(src, dst, to):
        at = len(copies)
        copy = pltpu.make_async_remote_copy(
            src, dst, send_sem.at[at], recv_sem.at[at], device_id=to, device_id_type=MESH
        )
        copy.start()
        copies.append(copy)

    loads[0].wait()
    loads[1].wait()
    row_src = {1: pl.ds(64, 8), -1: pl.ds(8, 8), 0: mid}
    row_dst = {1: pl.ds(0, 8), -1: pl.ds(72, 8), 0: mid}
    lane_src = {1: pl.ds(HALF, 128), -1: pl.ds(128, 128), 0: pl.ds(128, HALF)}
    lane_dst = {1: pl.ds(0, 128), -1: pl.ds(HALF + 128, 128), 0: pl.ds(128, HALF)}
    for dx, db in near:
        send(
            raw.at[:, row_src[dx], lane_src[db]],
            raw.at[:, row_dst[dx], lane_dst[db]],
            device(dx, db),
        )
    raw_copies = list(copies)

    send(vol_hbm.at[edge], vol.at[ghost, mid, pl.ds(128, WIDE)], partner)
    for by, src, dst in ((1, pl.ds(56, 8), pl.ds(0, 8)), (-1, pl.ds(0, 8), pl.ds(72, 8))):
        to = device(by, 0)
        across = device(by, side)
        send(seabed_hbm.at[src], seabed.at[dst, pl.ds(128, WIDE)], to)
        send(
            vol_hbm.at[:, src], vol.at[pl.ds(1, LAYERS), dst, pl.ds(128, WIDE)], to
        )
        send(vol_hbm.at[edge, src], vol.at[ghost, dst, pl.ds(128, WIDE)], across)
    for by, src, dst in (
        (1, pl.ds(WIDE - 128, 128), pl.ds(0, 128)),
        (-1, pl.ds(0, 128), pl.ds(WIDE + 128, 128)),
    ):
        to = device(0, 2 * by)
        across = (gx, lax.rem(gy + by + 4, 4), 1 - gz)
        send(seabed_hbm.at[:, src], seabed.at[mid, dst], to)
        send(vol_hbm.at[:, :, src], vol.at[pl.ds(1, LAYERS), mid, dst], to)
        send(vol_hbm.at[edge, :, src], vol.at[ghost, mid, dst], across)

    for copy in raw_copies:
        copy.wait_recv()

    def tiles(ref, field, r):
        def rows(i):
            return ref[field, pl.ds(pl.multiple_of(8 * i, 8), 8), :]

        return rows(jnp.maximum(r - 1, 0)), rows(r), rows(jnp.minimum(r + 1, 9))

    @pl.loop(0, 10)
    def _(r):
        height, poten = tiles(raw, 0, r), tiles(raw, 1, r)
        rate_height, rate_poten = section(height, poten)
        at = pl.ds(pl.multiple_of(8 * r, 8), 8)
        one[0, at, :] = height[1] + TIME_STEP * rate_height
        one[1, at, :] = poten[1] + TIME_STEP * rate_poten

    @pl.loop(0, 10)
    def _(r):
        height, poten = tiles(one, 0, r), tiles(one, 1, r)
        rates = section(height, poten)
        at = pl.ds(pl.multiple_of(8 * r, 8), 8)
        for f in (0, 1):
            first = (height, poten)[f][1]
            value = 0.5 * (raw[f, at, :] + first + TIME_STEP * rates[f])
            new[f, at, pl.ds(own, HALF)] = value[:, 128 : 128 + HALF]
            new[f, at, pl.ds(outer, 128)] = jnp.where(
                gz == 0, value[:, :128], value[:, HALF + 128 :]
            )

    outs = [
        pltpu.make_async_copy(new.at[0, mid, pl.ds(own, HALF)], new_e_out, local_sem.at[4]),
        pltpu.make_async_copy(new.at[1, mid, pl.ds(own, HALF)], new_p_out, local_sem.at[5]),
    ]
    for out in outs:
        out.start()
    send(new.at[:, :, pl.ds(own, HALF)], new.at[:, :, pl.ds(own, HALF)], partner)
    send(new.at[:, :, pl.ds(outer, 128)], new.at[:, :, pl.ds(outer, 128)], partner)

    for load in loads[2:]:
        load.wait()
    for copy in copies[len(raw_copies) :]:
        copy.wait_recv()

    @pl.loop(0, 10)
    def _(r):
        at = pl.ds(pl.multiple_of(8 * r, 8), 8)
        bed = seabed[at, :].astype(jnp.float32) * DEPTH_UNIT
        depth[at, :] = bed
        column[at, :] = bed + new[0, at, :]

        @pl.when(gz == 0)
        def _():
            vol[0, at, :] = vol[1, at, :]

        @pl.when(gz == 1)
        def _():
            vol[9, at, :] = 2.0 * new[1, at, :] - vol[8, at, :]

    first_sigma = (8.0 * gz.astype(jnp.float32) + 0.5) * 0.0625

    def differences(load):
        def parts(lanes, back):
            return load(lanes, back)

        centre = load(0, STRIP)
        wide = load(-128, STRIP + 256)
        return centre, wide

    @pl.loop(0, 8)
    def _(r):
        row = pl.multiple_of(8 * r + 8, 8)

        @pl.loop(0, WIDE // STRIP)
        def _(s):
            lane = pl.multiple_of(s * STRIP, 128)

            def around(ref, layer):
                def rows(at, lanes):
                    at = pl.ds(at, 8)
                    return ref[at, lanes] if layer is None else ref[layer, at, lanes]

                inner = pl.ds(lane + 128, STRIP)
                wide = rows(row, pl.ds(lane, STRIP + 256))
                here = wide[:, 128 : 128 + STRIP]
                before, after = rows(row - 8, inner), rows(row + 8, inner)
                up, down = row_shift(before, here, after, 1), row_shift(before, here, after, -1)
                right = lane_shift(wide, 1)[:, 128 : 128 + STRIP]
                left = lane_shift(wide, -1)[:, 128 : 128 + STRIP]
                return here, up - down, right - left, (up + down) + (right + left)

            here, column_north, column_east, _ = around(column, None)
            _, depth_north, depth_east, _ = around(depth, None)
            inverse = 1.0 / here
            scale = 4.0 * inverse
            step_north = column_north * scale
            step_east = column_east * scale
            slope_north = depth_north * scale - first_sigma * step_north
            slope_east = depth_east * scale - first_sigma * step_east
            step_north = step_north * 0.0625
            step_east = step_east * 0.0625
            base = 64.0 * inverse * inverse
            below = around(vol, 0)
            middle = around(vol, 1)
            for k in range(LAYERS):
                above = around(vol, k + 2)
                weight = slope_north * slope_north + slope_east * slope_east + base
                four = 4.0 * middle[0]
                vertical = 4.0 * (above[0] + below[0]) - 2.0 * four
                lap_ref[k, pl.ds(row - 8, 8), pl.ds(lane, STRIP)] = (
                    (middle[3] - four)
                    + slope_north * (above[1] - below[1])
                    + slope_east * (above[2] - below[2])
                    + weight * vertical
                )
                slope_north = slope_north - step_north
                slope_east = slope_east - step_east
                below, middle = middle, above

    for out in outs:
        out.wait()
    for copy in copies:
        copy.wait_send()


def shards(elevation, surface_potential, seabed, interior_potential):
    copies = 8 + 1 + 6 + 6 + 2
    hbm = pl.BlockSpec(memory_space=pltpu.HBM)
    f32 = jnp.float32
    return pl.pallas_call(
        kernel,
        out_shape=(
            jax.ShapeDtypeStruct((ROWS, HALF), f32),
            jax.ShapeDtypeStruct((ROWS, HALF), f32),
            pltpu.VMEM((LAYERS, ROWS, WIDE), f32),
        ),
        in_specs=[hbm] * 4,
        out_specs=(hbm, hbm, pl.BlockSpec(memory_space=pltpu.VMEM)),
        scratch_shapes=[
            pltpu.VMEM((2, ROWS + 16, HALF + 256), f32),
            pltpu.VMEM((2, ROWS + 16, HALF + 256), f32),
            pltpu.VMEM((2, ROWS + 16, WIDE + 256), f32),
            pltpu.VMEM((ROWS + 16, WIDE + 256), jnp.int32),
            pltpu.VMEM((LAYERS + 2, ROWS + 16, WIDE + 256), f32),
            pltpu.VMEM((ROWS + 16, WIDE + 256), f32),
            pltpu.VMEM((ROWS + 16, WIDE + 256), f32),
            pltpu.SemaphoreType.DMA((6,)),
            pltpu.SemaphoreType.DMA((copies,)),
            pltpu.SemaphoreType.DMA((copies,)),
        ],
        compiler_params=pltpu.CompilerParams(
            collective_id=0, has_side_effects=True, vmem_limit_bytes=40 << 20
        ),
        name="wave_step",
    )(elevation, surface_potential, seabed, interior_potential)


def solution(mesh):
    return jax.shard_map(
        shards,
        mesh=mesh,
        in_specs=(P("gx", ("gy", "gz")), P("gx", ("gy", "gz")), P("gx", "gy"), P("gz", "gx", "gy")),
        out_specs=(P("gx", ("gy", "gz")), P("gx", ("gy", "gz")), P("gz", "gx", "gy")),
        check_vma=False,
    )
```

time: 147 us -> 67.4 us (0.46)
  the two profiles are of different devices: /device:TPU:6 before, /device:TPU:8 now
where the time goes in v1:
time: 67.4 us; the launch traced here: 67.1 us
  Pallas kernels  57.9 us (86%)
  local copies, waits for them, and re-layouts  8.54 us (13%)
    pallas_call x1, Pallas kernels, shards(): pl.pallas_call(kernel, out_shape=(jax.ShapeDtypeStruct((ROWS, HALF), f32)...  57.9 us
    unnamed x11, local copies, waits for them, and re-layouts  8.54 us

profile of v1, /device:TPU:8, one launch (start us, length us, event | category | flops | bytes accessed | tf_op | source)
XLA Modules:
  0.0 67.1 jit_solution(13836415038649625196)
XLA Ops:
  0.6 0.0 copy-start
  0.6 2.2 %copy-done = f32[8,64,2048]{2,1,0:T(8,128)S(1)} copy-done((f32[8,64,2048]{2,1,0:T(8,128)S(1)}, f32[8,64,2048]{2,1,0:T(8,128)}, u32[]{:S(2)}) %copy-start) | copy-done | bytes 4194328
  2.8 0.0 copy-start.1
  2.8 1.0 %copy-done.1 = s32[64,2048]{1,0:T(8,128)S(1)} copy-done((s32[64,2048]{1,0:T(8,128)S(1)}, s32[64,2048]{1,0:T(8,128)}, u32[]{:S(2)}) %copy-start.1) | copy-done | bytes 524312
  3.9 0.0 copy-start.2
  3.9 0.9 %copy-done.2 = f32[64,1024]{1,0:T(8,128)S(1)} copy-done((f32[64,1024]{1,0:T(8,128)S(1)}, f32[64,1024]{1,0:T(8,128)}, u32[]{:S(2)}) %copy-start.2) | copy-done | bytes 262168
  4.8 0.0 copy-start.3
  4.8 0.9 %copy-done.3 = f32[64,1024]{1,0:T(8,128)S(1)} copy-done((f32[64,1024]{1,0:T(8,128)S(1)}, f32[64,1024]{1,0:T(8,128)}, u32[]{:S(2)}) %copy-start.3) | copy-done | bytes 262168
  5.8 57.9 %wave_step.1 = (f32[64,1024]{1,0:T(8,128)S(1)}, f32[64,1024]{1,0:T(8,128)S(1)}, f32[8,64,2048]{2,1,0:T(8,128)S(1)}) custom-call(f32[64,1024]{1,0:T(8,128)S(1)} %copy-done.2, f32[64,1024]{1,0:T(8,128)S(1)} %copy-done.3, s32[64,2048]{1,0:T(8,128)S(1)} %copy-done.1, f32[8,64,2048]{2,1,0:T(8,128)S(1)} %copy-done), custom_call_target="tpu_custom_call" | custom-call | tf_op jit(solution)/shard_map/wave_step/pallas_call | solution.py:264
  63.7 2.0 %copy.10 = f32[8,64,2048]{2,1,0:T(8,128)} copy(f32[8,64,2048]{2,1,0:T(8,128)S(1)} %get-tuple-element.5) | data formatting | bytes 8388608
  65.7 0.7 %copy.11 = f32[64,1024]{1,0:T(8,128)} copy(f32[64,1024]{1,0:T(8,128)S(1)} %get-tuple-element.9) | data formatting | bytes 524288
  66.4 0.7 %copy.12 = f32[64,1024]{1,0:T(8,128)} copy(f32[64,1024]{1,0:T(8,128)S(1)} %get-tuple-element.10) | data formatting | bytes 524288
Async XLA Ops:
  0.6 2.2 %copy-start = (f32[8,64,2048]{2,1,0:T(8,128)S(1)}, f32[8,64,2048]{2,1,0:T(8,128)}, u32[]{:S(2)}) copy-start(f32[8,64,2048]{2,1,0:T(8,128)} %vol_hbm.1) | copy-start | bytes 12582916
  2.8 1.0 %copy-start.1 = (s32[64,2048]{1,0:T(8,128)S(1)}, s32[64,2048]{1,0:T(8,128)}, u32[]{:S(2)}) copy-start(s32[64,2048]{1,0:T(8,128)} %seabed_hbm.1) | copy-start | bytes 1572868
  3.9 0.9 %copy-start.2 = (f32[64,1024]{1,0:T(8,128)S(1)}, f32[64,1024]{1,0:T(8,128)}, u32[]{:S(2)}) copy-start(f32[64,1024]{1,0:T(8,128)} %e_hbm.1) | copy-start | bytes 786436
  4.8 0.9 %copy-start.3 = (f32[64,1024]{1,0:T(8,128)S(1)}, f32[64,1024]{1,0:T(8,128)}, u32[]{:S(2)}) copy-start(f32[64,1024]{1,0:T(8,128)} %p_hbm.1) | copy-start | bytes 786436

commit v2 on v1

v2 whole, which is shorter than its diff:
```python
import jax
import jax.numpy as jnp
from jax import lax
from jax.experimental import pallas as pl
from jax.experimental.pallas import tpu as pltpu
from jax.sharding import PartitionSpec as P

MESH = pl.DeviceIdType.MESH
TIME_STEP = 0.05
DEPTH_UNIT = 0.015625

ROWS = 64
HALF = 1024
WIDE = 2048
LAYERS = 8
STRIP = 512
EARLY = 40
COPIES = 32


def lane_shift(x, by):
    return pltpu.roll(x, (-by) % x.shape[-1], axis=len(x.shape) - 1)


def row_shift(before, here, after, by):
    rows = lax.broadcasted_iota(jnp.int32, here.shape, 0)
    moved = pltpu.roll(here, (-by) % 8, axis=0)
    if by > 0:
        return jnp.where(rows >= 8 - by, pltpu.roll(after, 8 - by, axis=0), moved)
    return jnp.where(rows < -by, pltpu.roll(before, -by, axis=0), moved)


def section(height, poten):
    def parts(tiles):
        before, here, after = tiles
        north = [row_shift(before, here, after, by) for by in (-2, -1, 1, 2)]
        east = [lane_shift(here, by) for by in (-2, -1, 1, 2)]
        return north, east

    def first(m2, m1, p1, p2):
        return 8.0 * (p1 - m1) - (p2 - m2)

    height_north, height_east = parts(height)
    poten_north, poten_east = parts(poten)
    e_n, e_e = first(*height_north), first(*height_east)
    p_n, p_e = first(*poten_north), first(*poten_east)
    near = (poten_north[1] + poten_north[2]) + (poten_east[1] + poten_east[2])
    far = (poten_north[0] + poten_north[3]) + (poten_east[0] + poten_east[3])
    curve = 16.0 * near - far - 60.0 * poten[1]
    rate_height = curve * (1.0 / 12.0) - (e_n * p_n + e_e * p_e) * (1.0 / 144.0)
    rate_poten = -height[1] - (p_n * p_n + p_e * p_e) * (0.5 / 144.0)
    return rate_height, rate_poten


def kernel(
    e_hbm, p_hbm, seabed_hbm, vol_hbm,
    new_e_out, new_p_out, lap_ref,
    raw, one, new, seabed, vol, depth, column,
    side_x, side_send, side_recv, side_in,
    rows_out, rows_in, ring_rows, new_rows_out, new_rows_in, cols_out, cols_in,
    local_sem, send_sem, recv_sem,
):
    gx, gy, gz = lax.axis_index("gx"), lax.axis_index("gy"), lax.axis_index("gz")
    block = 2 * gy + gz

    def device(dx, db):
        at = lax.rem(block + db + 8, 8)
        return (lax.rem(gx + dx + 32, 32), lax.div(at, 2), lax.rem(at, 2))

    side = 1 - 2 * gz
    partner = (gx, gy, 1 - gz)
    theirs = 9 * gz
    mine = 9 - theirs
    edge = 7 * (1 - gz)
    mid = pl.ds(8, ROWS)
    inner = pl.ds(128, HALF)
    tile = pl.ds(128, WIDE)

    loads = [
        pltpu.make_async_copy(e_hbm, raw.at[0, mid, inner], local_sem.at[0]),
        pltpu.make_async_copy(p_hbm, raw.at[1, mid, inner], local_sem.at[1]),
        pltpu.make_async_copy(seabed_hbm, seabed.at[:, tile], local_sem.at[2]),
        pltpu.make_async_copy(vol_hbm, vol.at[pl.ds(1, LAYERS), mid, tile], local_sem.at[3]),
    ]
    for load in loads:
        load.start()

    barrier = pltpu.get_barrier_semaphore()
    corners = [(-1, -1), (-1, 1), (1, -1), (1, 1)]
    for dx, db in corners + [(-1, 0), (1, 0), (0, -1), (0, 1), (0, -2), (0, 2)]:
        pl.semaphore_signal(barrier, inc=1, device_id=device(dx, db), device_id_type=MESH)

    lanes = lax.broadcasted_iota(jnp.int32, (ROWS, 128), 1)
    loads[0].wait()
    loads[1].wait()
    e_side, p_side = raw[0, mid, pl.ds(HALF, 128)], raw[1, mid, pl.ds(HALF, 128)]
    side_x[0] = jnp.where(lanes < 8, pltpu.roll(e_side, 8, axis=1), pltpu.roll(p_side, 16, axis=1))
    e_side, p_side = raw[0, mid, pl.ds(128, 128)], raw[1, mid, pl.ds(128, 128)]
    side_x[1] = jnp.where(lanes < 8, e_side, pltpu.roll(p_side, 8, axis=1))
    for d in (0, 1):
        side_send[d, :, pl.ds(0, ROWS)] = jnp.transpose(side_x[d])[:16]

    pl.semaphore_wait(barrier, 10)

    started = []

    def message(src, dst, to):
        at = len(started)
        assert at < COPIES
        copy = pltpu.make_async_remote_copy(
            src, dst, send_sem.at[at], recv_sem.at[at], device_id=to, device_id_type=MESH
        )
        started.append(copy)
        return copy

    def send(src, dst, to):
        copy = message(src, dst, to)
        copy.start()
        return copy

    raw_copies = []
    for d, db in ((0, 1), (1, -1)):
        raw_copies.append(send(side_send.at[d], side_recv.at[d], device(0, db)))
        for dx, src, dst in ((1, pl.ds(56, 8), pl.ds(0, 8)), (-1, pl.ds(0, 8), pl.ds(72, 8))):
            raw_copies.append(send(side_x.at[d, src], side_in.at[d, dst], device(dx, db)))
    for dx, src, dst in ((1, pl.ds(64, 8), pl.ds(0, 8)), (-1, pl.ds(8, 8), pl.ds(72, 8))):
        raw_copies.append(send(raw.at[:, src, inner], raw.at[:, dst, inner], device(dx, 0)))

    bound_early = send(
        vol_hbm.at[edge, pl.ds(0, EARLY)], vol.at[theirs, pl.ds(8, EARLY), tile], partner
    )
    bound_late = message(
        vol_hbm.at[edge, pl.ds(EARLY, ROWS - EARLY)],
        vol.at[theirs, pl.ds(8 + EARLY, ROWS - EARLY), tile],
        partner,
    )
    side_copies = []
    for by, src, dst in (
        (1, pl.ds(WIDE - 128, 128), pl.ds(0, 128)),
        (-1, pl.ds(0, 128), pl.ds(WIDE + 128, 128)),
    ):
        to = device(0, 2 * by)
        side_copies.append(send(vol_hbm.at[:, :, src], vol.at[pl.ds(1, LAYERS), mid, dst], to))
        side_copies.append(send(seabed_hbm.at[:, src], seabed.at[:, dst], to))

    loads[2].wait()
    loads[3].wait()
    for d, row in ((0, 63), (1, 0)):

        @pl.loop(0, LAYERS)
        def _(k):
            for t in range(16):
                rows_out[d, k, pl.ds(t, 1), :] = vol[
                    k + 1, pl.ds(row + 8, 1), pl.ds(128 + 128 * t, 128)
                ]

        for t in range(16):
            bed = seabed[pl.ds(row, 1), pl.ds(128 + 128 * t, 128)]
            rows_out[d, LAYERS, pl.ds(t, 1), :] = bed.astype(jnp.float32) * DEPTH_UNIT
    row_copies = []
    for d, dx in ((0, 1), (1, -1)):
        row_copies.append(send(rows_out.at[d], rows_in.at[d], device(dx, 0)))
        row_copies.append(send(rows_out.at[d, edge], ring_rows.at[d], device(dx, side)))

    for copy in raw_copies:
        copy.wait_recv()
    for d in (0, 1):
        back = jnp.transpose(side_recv[d])
        side_in[d, mid, pl.ds(0, 16)] = back[:ROWS]
        block_in = side_in[d]
        at = pl.ds(0, 128) if d == 0 else pl.ds(HALF + 128, 128)
        raw[0, :, at] = pltpu.roll(block_in, 120, axis=1) if d == 0 else block_in
        raw[1, :, at] = pltpu.roll(block_in, 112 if d == 0 else 120, axis=1)

    def tiles(ref, lead, r):
        def rows(i):
            return ref[lead + (pl.ds(pl.multiple_of(8 * i, 8), 8), slice(None))]

        return rows(jnp.maximum(r - 1, 0)), rows(r), rows(jnp.minimum(r + 1, 9))

    @pl.loop(0, 10)
    def _(r):
        height, poten = tiles(raw, (0,), r), tiles(raw, (1,), r)
        rate_height, rate_poten = section(height, poten)
        at = pl.ds(pl.multiple_of(8 * r, 8), 8)
        one[0, at, :] = height[1] + TIME_STEP * rate_height
        one[1, at, :] = poten[1] + TIME_STEP * rate_poten

    @pl.loop(0, 10)
    def _(r):
        height, poten = tiles(one, (0,), r), tiles(one, (1,), r)
        rates = section(height, poten)
        at = pl.ds(pl.multiple_of(8 * r, 8), 8)
        for f in (0, 1):
            first = (height, poten)[f][1]
            new[0, f, at, :] = 0.5 * (raw[f, at, :] + first + TIME_STEP * rates[f])

    field_copies = [
        message(new.at[0, f, mid, inner], new.at[1, f, mid, inner], partner) for f in (0, 1)
    ]
    field_copies[0].start()

    @pl.when(gz == 0)
    def _():
        field_copies[1].start()

    for f in (0, 1):
        for d, row in ((0, 7), (1, 72)):
            for t in range(8):
                new_rows_out[f, d, pl.ds(t, 1), :] = new[
                    0, f, pl.ds(row, 1), pl.ds(128 + 128 * t, 128)
                ]
    ring_copies = [send(new_rows_out, new_rows_in, partner)]
    new_e_out[...] = new[0, 0, mid, inner]
    new_p_out[...] = new[0, 1, mid, inner]

    for copy in side_copies:
        copy.wait_recv()
    outer = pl.multiple_of((HALF + 128) * gz, 128)
    left = vol[edge + 1, mid, pl.ds(0, 128)]
    right = vol[edge + 1, mid, pl.ds(WIDE + 128, 128)]
    outer_e = new[0, 0, mid, pl.ds(outer, 128)]
    outer_p = new[0, 1, mid, pl.ds(outer, 128)]

    def pick(x, even, odd):
        return jnp.where(
            gz == 0, pltpu.roll(x, even, axis=1), pltpu.roll(x, odd, axis=1)
        )

    packed = jnp.where(
        lanes < 2,
        jnp.where(lanes == 0, pltpu.roll(left, 1, axis=1), pltpu.roll(right, 1, axis=1)),
        jnp.where(lanes == 2, pick(outer_e, 3, 2), pick(outer_p, 4, 3)),
    )
    cols_out[:, pl.ds(0, ROWS)] = jnp.transpose(packed)[:8]
    ring_copies.append(send(cols_out, cols_in, partner))

    @pl.loop(0, 8)
    def _(r):
        at = pl.multiple_of(8 * r, 8)
        depth[pl.ds(at + 8, 8), :] = seabed[pl.ds(at, 8), :].astype(jnp.float32) * DEPTH_UNIT

    for copy in row_copies:
        copy.wait_recv()
    for d, row in ((0, 7), (1, 72)):

        @pl.loop(0, LAYERS)
        def _(k):
            for t in range(16):
                vol[k + 1, pl.ds(row, 1), pl.ds(128 + 128 * t, 128)] = rows_in[d, k, pl.ds(t, 1), :]

        for t in range(16):
            at = pl.ds(128 + 128 * t, 128)
            depth[pl.ds(row, 1), at] = rows_in[d, LAYERS, pl.ds(t, 1), :]
            vol[mine, pl.ds(row, 1), at] = ring_rows[d, pl.ds(t, 1), :]

    def prepare(h):
        base = pl.multiple_of(HALF * (gz if h == 0 else 1 - gz), 128)
        span = pl.ds(base, HALF + 256)

        @pl.loop(0, 10)
        def _(r):
            at = pl.ds(pl.multiple_of(8 * r, 8), 8)
            column[h, at, :] = depth[at, span] + new[h, 0, at, :]

            @pl.when(gz == 0)
            def _():
                vol[0, at, span] = vol[1, at, span]

            @pl.when(gz == 1)
            def _():
                vol[9, at, span] = 2.0 * new[h, 1, at, :] - vol[8, at, span]

    def laplace(h, start, count, first_tile, last_tile):
        base = HALF * (gz if h == 0 else 1 - gz)
        sigma = ((8 * gz + start).astype(jnp.float32) + 0.5) * 0.0625

        @pl.loop(first_tile, last_tile)
        def _(r):
            row = pl.multiple_of(8 * r + 8, 8)

            @pl.loop(0, HALF // STRIP)
            def _(s):
                lane = pl.multiple_of(s * STRIP, 128)
                full = pl.multiple_of(base + lane, 128)

                def around(ref, lead, lane):
                    def rows(at, lanes):
                        return ref[lead + (pl.ds(at, 8), lanes)]

                    wide = rows(row, pl.ds(lane, STRIP + 256))
                    here = wide[:, 128 : 128 + STRIP]
                    centre = pl.ds(pl.multiple_of(lane + 128, 128), STRIP)
                    before, after = rows(row - 8, centre), rows(row + 8, centre)
                    up = row_shift(before, here, after, 1)
                    down = row_shift(before, here, after, -1)
                    right = lane_shift(wide, 1)[:, 128 : 128 + STRIP]
                    left = lane_shift(wide, -1)[:, 128 : 128 + STRIP]
                    return here, up - down, right - left, (up + down) + (right + left)

                here, column_north, column_east, _ = around(column, (h,), lane)
                _, depth_north, depth_east, _ = around(depth, (), full)
                inverse = 1.0 / here
                scale = 4.0 * inverse
                step_north = column_north * scale
                step_east = column_east * scale
                slope_north = depth_north * scale - sigma * step_north
                slope_east = depth_east * scale - sigma * step_east
                step_north = step_north * 0.0625
                step_east = step_east * 0.0625
                bottom = 64.0 * inverse * inverse
                below = around(vol, (start,), full)
                middle = around(vol, (start + 1,), full)
                for k in range(count):
                    above = around(vol, (start + k + 2,), full)
                    weight = slope_north * slope_north + slope_east * slope_east + bottom
                    four = 4.0 * middle[0]
                    vertical = 4.0 * (above[0] + below[0]) - 2.0 * four
                    lap_ref[start + k, pl.ds(row - 8, 8), pl.ds(full, STRIP)] = (
                        (middle[3] - four)
                        + slope_north * (above[1] - below[1])
                        + slope_east * (above[2] - below[2])
                        + weight * vertical
                    )
                    slope_north = slope_north - step_north
                    slope_east = slope_east - step_east
                    below, middle = middle, above

    prepare(0)
    laplace(0, gz, LAYERS - 1, 0, 8)

    @pl.when(gz == 1)
    def _():
        field_copies[0].wait_send()
        bound_late.start()
        field_copies[1].wait_recv()

    field_copies[0].wait_recv()
    for copy in ring_copies:
        copy.wait_recv()
    for f in (0, 1):
        for d, row in ((0, 7), (1, 72)):
            for t in range(8):
                new[1, f, pl.ds(row, 1), pl.ds(128 + 128 * t, 128)] = new_rows_in[
                    f, d, pl.ds(t, 1), :
                ]
    back = jnp.transpose(cols_in[...])[:ROWS]
    seam = jnp.zeros((ROWS, 128 - 8), jnp.float32)
    back = jnp.concatenate([back, seam], axis=1)
    vol[mine, mid, pl.ds(0, 128)] = pltpu.roll(back, 127, axis=1)
    vol[mine, mid, pl.ds(WIDE + 128, 128)] = pltpu.roll(back, 127, axis=1)
    far = pl.multiple_of((HALF + 128) * (1 - gz), 128)
    close = pl.multiple_of((HALF + 128) * gz, 128)
    inside = pl.multiple_of(HALF * (1 - gz) + 128 * gz, 128)
    for f in (0, 1):
        new[1, f, mid, pl.ds(far, 128)] = pick(back, 126 - f, 125 - f)
        new[1, f, mid, pl.ds(close, 128)] = new[0, f, mid, pl.ds(inside, 128)]

    prepare(1)
    laplace(1, gz, LAYERS - 1, 0, 8)

    @pl.when(gz == 0)
    def _():
        field_copies[0].wait_send()
        field_copies[1].wait_send()
        bound_late.start()

    bound_early.wait_recv()
    split = EARLY // 8 - 1
    for h in (0, 1):
        laplace(h, edge, 1, 0, split)
    bound_late.wait_recv()
    for h in (0, 1):
        laplace(h, edge, 1, split, 8)

    for copy in started:
        if all(copy is not other for other in field_copies):
            copy.wait_send()


def write(e_ref, p_ref, lap_ref, e_out, p_out, lap_out, sem):
    copies = [
        pltpu.make_async_copy(src, dst, sem.at[i])
        for i, (src, dst) in enumerate(((lap_ref, lap_out), (e_ref, e_out), (p_ref, p_out)))
    ]
    for copy in copies:
        copy.start()
    for copy in copies:
        copy.wait()


def shards(elevation, surface_potential, seabed, interior_potential):
    hbm = pl.BlockSpec(memory_space=pltpu.HBM)
    vmem = pl.BlockSpec(memory_space=pltpu.VMEM)
    f32 = jnp.float32
    held = (
        pltpu.VMEM((ROWS, HALF), f32),
        pltpu.VMEM((ROWS, HALF), f32),
        pltpu.VMEM((LAYERS, ROWS, WIDE), f32),
    )
    operands = [
        pltpu.with_memory_space_constraint(x, pltpu.HBM)
        for x in (elevation, surface_potential, seabed, interior_potential)
    ]
    results = pl.pallas_call(
        kernel,
        out_shape=held,
        in_specs=[hbm] * 4,
        out_specs=(vmem,) * 3,
        scratch_shapes=[
            pltpu.VMEM((2, ROWS + 16, HALF + 256), f32),
            pltpu.VMEM((2, ROWS + 16, HALF + 256), f32),
            pltpu.VMEM((2, 2, ROWS + 16, HALF + 256), f32),
            pltpu.VMEM((ROWS, WIDE + 256), jnp.int32),
            pltpu.VMEM((LAYERS + 2, ROWS + 16, WIDE + 256), f32),
            pltpu.VMEM((ROWS + 16, WIDE + 256), f32),
            pltpu.VMEM((2, ROWS + 16, HALF + 256), f32),
            pltpu.VMEM((2, ROWS, 128), f32),
            pltpu.VMEM((2, 16, 128), f32),
            pltpu.VMEM((2, 16, 128), f32),
            pltpu.VMEM((2, ROWS + 16, 128), f32),
            pltpu.VMEM((2, LAYERS + 1, 16, 128), f32),
            pltpu.VMEM((2, LAYERS + 1, 16, 128), f32),
            pltpu.VMEM((2, 16, 128), f32),
            pltpu.VMEM((2, 2, 8, 128), f32),
            pltpu.VMEM((2, 2, 8, 128), f32),
            pltpu.VMEM((8, 128), f32),
            pltpu.VMEM((8, 128), f32),
            pltpu.SemaphoreType.DMA((4,)),
            pltpu.SemaphoreType.DMA((COPIES,)),
            pltpu.SemaphoreType.DMA((COPIES,)),
        ],
        compiler_params=pltpu.CompilerParams(
            collective_id=0, has_side_effects=True, vmem_limit_bytes=40 << 20
        ),
        name="wave_step",
    )(*operands)
    return pl.pallas_call(
        write,
        out_shape=tuple(jax.ShapeDtypeStruct(x.shape, f32) for x in results),
        in_specs=[vmem] * 3,
        out_specs=(hbm,) * 3,
        scratch_shapes=[pltpu.SemaphoreType.DMA((3,))],
        compiler_params=pltpu.CompilerParams(vmem_limit_bytes=4 << 20),
        name="write_results",
    )(*(pltpu.with_memory_space_constraint(x, pltpu.VMEM) for x in results))


def solution(mesh):
    return jax.shard_map(
        shards,
        mesh=mesh,
        in_specs=(P("gx", ("gy", "gz")), P("gx", ("gy", "gz")), P("gx", "gy"), P("gz", "gx", "gy")),
        out_specs=(P("gx", ("gy", "gz")), P("gx", ("gy", "gz")), P("gz", "gx", "gy")),
        check_vma=False,
    )
```

time: 67.4 us -> 41 us (0.61)
  Pallas kernels: 57.9 us -> 40.2 us
  local copies, waits for them, and re-layouts: 8.54 us -> 0 us
    pallas_call x1 -> x2, Pallas kernels: 57.9 us -> 40.2 us  [the longest x1 38.1 us: shards(): pl.pallas_call(kernel, out_shape=held, in_specs=[hbm] * 4, out_specs=(vme...]
    unnamed x11 -> x0, local copies, waits for them, and re-layouts: 8.54 us -> none
where the time goes in v2:
time: 41 us; the launch traced here: 40.9 us
  Pallas kernels  40.2 us (98%)
  between operations  0.64 us (2%)
    pallas_call x1, Pallas kernels, shards(): pl.pallas_call(kernel, out_shape=held, in_specs=[hbm] * 4, out_specs=(vme...  38.1 us
    pallas_call x1, Pallas kernels, shards(): pl.pallas_call(write, out_shape=tuple((jax.ShapeDtypeStruct(x.shape, f32)...  2.19 us

profile of v2, /device:TPU:8, one launch (start us, length us, event | category | flops | bytes accessed | tf_op | source)
XLA Modules:
  0.0 40.9 jit_solution(6767678094571049854)
XLA Ops:
  0.6 38.1 %wave_step.1 = (f32[64,1024]{1,0:T(8,128)S(1)}, f32[64,1024]{1,0:T(8,128)S(1)}, f32[8,64,2048]{2,1,0:T(8,128)S(1)}) custom-call(f32[64,1024]{1,0:T(8,128)} %e_hbm.1, f32[64,1024]{1,0:T(8,128)} %p_hbm.1, s32[64,2048]{1,0:T(8,128)} %seabed_hbm.1, f32[8,64,2048]{2,1,0:T(8,128)} %vol_hbm.1), custom_call_target="tpu_custom_call" | custom-call | tf_op jit(solution)/shard_map/wave_step/pallas_call | solution.py:405
  38.7 2.2 %write_results.1 = (f32[64,1024]{1,0:T(8,128)}, f32[64,1024]{1,0:T(8,128)}, f32[8,64,2048]{2,1,0:T(8,128)}) custom-call(f32[64,1024]{1,0:T(8,128)S(1)} %get-tuple-element.6.e_ref, f32[64,1024]{1,0:T(8,128)S(1)} %get-tuple-element.7.p_ref, f32[8,64,2048]{2,1,0:T(8,128)S(1)} %get-tuple-element.8.lap_ref), custom_call_target="tpu_custom_call" | custom-call | tf_op jit(solution)/shard_map/write_results/pallas_call | solution.py:438

commit v3 on v2

--- a/solution.py
+++ b/solution.py
@@ -13,7 +13,7 @@
 HALF = 1024
 WIDE = 2048
 LAYERS = 8
-STRIP = 512
+STRIP = 1024
 EARLY = 40
 COPIES = 32
 
@@ -56,7 +56,7 @@
     e_hbm, p_hbm, seabed_hbm, vol_hbm,
     new_e_out, new_p_out, lap_ref,
     raw, one, new, seabed, vol, depth, column,
-    side_x, side_send, side_recv, side_in,
+    side_x, side_send, side_recv, side_in, relay, relay_two,
     rows_out, rows_in, ring_rows, new_rows_out, new_rows_in, cols_out, cols_in,
     local_sem, send_sem, recv_sem,
 ):
@@ -69,6 +69,7 @@
 
     side = 1 - 2 * gz
     partner = (gx, gy, 1 - gz)
+    opposite = (lax.rem(gx + 16, 32), gy, 1 - gz)
     theirs = 9 * gz
     mine = 9 - theirs
     edge = 7 * (1 - gz)
@@ -89,6 +90,7 @@
     corners = [(-1, -1), (-1, 1), (1, -1), (1, 1)]
     for dx, db in corners + [(-1, 0), (1, 0), (0, -1), (0, 1), (0, -2), (0, 2)]:
         pl.semaphore_signal(barrier, inc=1, device_id=device(dx, db), device_id_type=MESH)
+    pl.semaphore_signal(barrier, inc=1, device_id=opposite, device_id_type=MESH)
 
     lanes = lax.broadcasted_iota(jnp.int32, (ROWS, 128), 1)
     loads[0].wait()
@@ -100,23 +102,25 @@
     for d in (0, 1):
         side_send[d, :, pl.ds(0, ROWS)] = jnp.transpose(side_x[d])[:16]
 
-    pl.semaphore_wait(barrier, 10)
-
-    started = []
+    pl.semaphore_wait(barrier, 11)
+
+    started, made = [], []
 
     def message(src, dst, to):
-        at = len(started)
+        at = len(made)
         assert at < COPIES
         copy = pltpu.make_async_remote_copy(
             src, dst, send_sem.at[at], recv_sem.at[at], device_id=to, device_id_type=MESH
         )
-        started.append(copy)
+        made.append(copy)
         return copy
 
     def send(src, dst, to):
         copy = message(src, dst, to)
         copy.start()
+        started.append(copy)
         return copy
+
 
     raw_copies = []
     for d, db in ((0, 1), (1, -1)):
@@ -126,14 +130,22 @@
     for dx, src, dst in ((1, pl.ds(64, 8), pl.ds(0, 8)), (-1, pl.ds(8, 8), pl.ds(72, 8))):
         raw_copies.append(send(raw.at[:, src, inner], raw.at[:, dst, inner], device(dx, 0)))
 
+    rest = pl.ds(EARLY, ROWS - EARLY)
+    rest_in = pl.ds(8 + EARLY, ROWS - EARLY)
     bound_early = send(
         vol_hbm.at[edge, pl.ds(0, EARLY)], vol.at[theirs, pl.ds(8, EARLY), tile], partner
     )
-    bound_late = message(
-        vol_hbm.at[edge, pl.ds(EARLY, ROWS - EARLY)],
-        vol.at[theirs, pl.ds(8 + EARLY, ROWS - EARLY), tile],
-        partner,
-    )
+    bound_late = message(vol_hbm.at[0, rest], vol.at[9, rest_in, tile], partner)
+    hops = [
+        message(vol_hbm.at[7, rest], relay, opposite),
+        message(relay, relay_two, partner),
+        message(relay_two, vol.at[0, rest_in, tile], opposite),
+    ]
+
+    @pl.when(gz == 0)
+    def _():
+        hops[0].start()
+
     side_copies = []
     for by, src, dst in (
         (1, pl.ds(WIDE - 128, 128), pl.ds(0, 128)),
@@ -186,6 +198,11 @@
         one[0, at, :] = height[1] + TIME_STEP * rate_height
         one[1, at, :] = poten[1] + TIME_STEP * rate_poten
 
+    @pl.when(gz == 1)
+    def _():
+        hops[0].wait_recv()
+        hops[1].start()
+
     @pl.loop(0, 10)
     def _(r):
         height, poten = tiles(one, (0,), r), tiles(one, (1,), r)
@@ -199,10 +216,6 @@
         message(new.at[0, f, mid, inner], new.at[1, f, mid, inner], partner) for f in (0, 1)
     ]
     field_copies[0].start()
-
-    @pl.when(gz == 0)
-    def _():
-        field_copies[1].start()
 
     for f in (0, 1):
         for d, row in ((0, 7), (1, 72)):
@@ -252,24 +265,26 @@
         for t in range(16):
             at = pl.ds(128 + 128 * t, 128)
             depth[pl.ds(row, 1), at] = rows_in[d, LAYERS, pl.ds(t, 1), :]
-            vol[mine, pl.ds(row, 1), at] = ring_rows[d, pl.ds(t, 1), :]
-
-    def prepare(h):
+
+    def prepare(h, do_column, do_top):
         base = pl.multiple_of(HALF * (gz if h == 0 else 1 - gz), 128)
         span = pl.ds(base, HALF + 256)
 
         @pl.loop(0, 10)
         def _(r):
             at = pl.ds(pl.multiple_of(8 * r, 8), 8)
-            column[h, at, :] = depth[at, span] + new[h, 0, at, :]
-
-            @pl.when(gz == 0)
-            def _():
-                vol[0, at, span] = vol[1, at, span]
-
-            @pl.when(gz == 1)
-            def _():
-                vol[9, at, span] = 2.0 * new[h, 1, at, :] - vol[8, at, span]
+            if do_column:
+                column[h, at, :] = depth[at, span] + new[h, 0, at, :]
+
+                @pl.when(gz == 0)
+                def _():
+                    vol[0, at, span] = vol[1, at, span]
+
+            if do_top:
+
+                @pl.when(gz == 1)
+                def _():
+                    vol[9, at, span] = 2.0 * new[h, 1, at, :] - vol[8, at, span]
 
     def laplace(h, start, count, first_tile, last_tile):
         base = HALF * (gz if h == 0 else 1 - gz)
@@ -326,27 +341,27 @@
                     slope_east = slope_east - step_east
                     below, middle = middle, above
 
-    prepare(0)
+    prepare(0, True, True)
     laplace(0, gz, LAYERS - 1, 0, 8)
 
-    @pl.when(gz == 1)
-    def _():
-        field_copies[0].wait_send()
-        bound_late.start()
-        field_copies[1].wait_recv()
-
-    field_copies[0].wait_recv()
+    @pl.when(gz == 0)
+    def _():
+        field_copies[1].start()
+        hops[1].wait_recv()
+        hops[2].start()
+
     for copy in ring_copies:
         copy.wait_recv()
-    for f in (0, 1):
-        for d, row in ((0, 7), (1, 72)):
+    for d, row in ((0, 7), (1, 72)):
+        for t in range(16):
+            vol[mine, pl.ds(row, 1), pl.ds(128 + 128 * t, 128)] = ring_rows[d, pl.ds(t, 1), :]
+        for f in (0, 1):
             for t in range(8):
                 new[1, f, pl.ds(row, 1), pl.ds(128 + 128 * t, 128)] = new_rows_in[
                     f, d, pl.ds(t, 1), :
                 ]
     back = jnp.transpose(cols_in[...])[:ROWS]
-    seam = jnp.zeros((ROWS, 128 - 8), jnp.float32)
-    back = jnp.concatenate([back, seam], axis=1)
+    back = jnp.concatenate([back, jnp.zeros((ROWS, 128 - 8), jnp.float32)], axis=1)
     vol[mine, mid, pl.ds(0, 128)] = pltpu.roll(back, 127, axis=1)
     vol[mine, mid, pl.ds(WIDE + 128, 128)] = pltpu.roll(back, 127, axis=1)
     far = pl.multiple_of((HALF + 128) * (1 - gz), 128)
@@ -356,26 +371,49 @@
         new[1, f, mid, pl.ds(far, 128)] = pick(back, 126 - f, 125 - f)
         new[1, f, mid, pl.ds(close, 128)] = new[0, f, mid, pl.ds(inside, 128)]
 
-    prepare(1)
-    laplace(1, gz, LAYERS - 1, 0, 8)
-
-    @pl.when(gz == 0)
-    def _():
-        field_copies[0].wait_send()
-        field_copies[1].wait_send()
-        bound_late.start()
-
     bound_early.wait_recv()
     split = EARLY // 8 - 1
-    for h in (0, 1):
-        laplace(h, edge, 1, 0, split)
-    bound_late.wait_recv()
-    for h in (0, 1):
-        laplace(h, edge, 1, split, 8)
+    laplace(0, edge, 1, 0, split)
+
+    @pl.when(gz == 1)
+    def _():
+        field_copies[0].wait_send()
+        bound_late.start()
+
+    field_copies[0].wait_recv()
+    prepare(1, True, False)
+
+    @pl.when(gz == 0)
+    def _():
+        laplace(1, 0, LAYERS - 1, 0, 8)
+        laplace(1, LAYERS - 1, 1, 0, split)
+        bound_late.wait_recv()
+        for h in (0, 1):
+            laplace(h, LAYERS - 1, 1, split, 8)
+
+    @pl.when(gz == 1)
+    def _():
+        laplace(1, 1, LAYERS - 2, 0, 8)
+        laplace(1, 0, 1, 0, split)
+        hops[2].wait_recv()
+        for h in (0, 1):
+            laplace(h, 0, 1, split, 8)
+        field_copies[1].wait_recv()
+        prepare(1, False, True)
+        laplace(1, LAYERS - 1, 1, 0, 8)
+
+    @pl.when(gz == 0)
+    def _():
+        for copy in (*field_copies, hops[0], hops[2]):
+            copy.wait_send()
+
+    @pl.when(gz == 1)
+    def _():
+        for copy in (hops[1], bound_late):
+            copy.wait_send()
 
     for copy in started:
-        if all(copy is not other for other in field_copies):
-            copy.wait_send()
+        copy.wait_send()
 
 
 def write(e_ref, p_ref, lap_ref, e_out, p_out, lap_out, sem):
@@ -419,6 +457,8 @@
             pltpu.VMEM((2, 16, 128), f32),
             pltpu.VMEM((2, 16, 128), f32),
             pltpu.VMEM((2, ROWS + 16, 128), f32),
+            pltpu.VMEM((ROWS - EARLY, WIDE), f32),
+            pltpu.VMEM((ROWS - EARLY, WIDE), f32),
             pltpu.VMEM((2, LAYERS + 1, 16, 128), f32),
             pltpu.VMEM((2, LAYERS + 1, 16, 128), f32),
             pltpu.VMEM((2, 16, 128), f32),

time: 41 us -> 37.4 us (0.912); the launches traced: 40.9 us -> 36.7 us
  Pallas kernels: 40.2 us -> 36 us
    pallas_call x1, Pallas kernels: 38.1 us -> 33.9 us  [shards(): pl.pallas_call(kernel, out_shape=held, in_specs=[hbm] * 4, out_specs=(vme...]
where the time goes in v3:
time: 37.4 us; the launch traced here: 36.7 us
  Pallas kernels  36 us (96%)
  between operations  0.64 us (2%)
    pallas_call x1, Pallas kernels, shards(): pl.pallas_call(kernel, out_shape=held, in_specs=[hbm] * 4, out_specs=(vme...  33.9 us
    pallas_call x1, Pallas kernels, shards(): pl.pallas_call(write, out_shape=tuple((jax.ShapeDtypeStruct(x.shape, f32)...  2.19 us

profile of v3, /device:TPU:8, one launch (start us, length us, event | category | flops | bytes accessed | tf_op | source)
XLA Modules:
  0.0 36.7 jit_solution(8616726164224861078)
XLA Ops:
  0.6 33.9 %wave_step.1 = (f32[64,1024]{1,0:T(8,128)S(1)}, f32[64,1024]{1,0:T(8,128)S(1)}, f32[8,64,2048]{2,1,0:T(8,128)S(1)}) custom-call(f32[64,1024]{1,0:T(8,128)} %e_hbm.1, f32[64,1024]{1,0:T(8,128)} %p_hbm.1, s32[64,2048]{1,0:T(8,128)} %seabed_hbm.1, f32[8,64,2048]{2,1,0:T(8,128)} %vol_hbm.1), custom_call_target="tpu_custom_call" | custom-call | tf_op jit(solution)/shard_map/wave_step/pallas_call | solution.py:443
  34.5 2.2 %write_results.1 = (f32[64,1024]{1,0:T(8,128)}, f32[64,1024]{1,0:T(8,128)}, f32[8,64,2048]{2,1,0:T(8,128)}) custom-call(f32[64,1024]{1,0:T(8,128)S(1)} %get-tuple-element.6.e_ref, f32[64,1024]{1,0:T(8,128)S(1)} %get-tuple-element.7.p_ref, f32[8,64,2048]{2,1,0:T(8,128)S(1)} %get-tuple-element.8.lap_ref), custom_call_target="tpu_custom_call" | custom-call | tf_op jit(solution)/shard_map/write_results/pallas_call | solution.py:478

commit v4 on v3

--- a/solution.py
+++ b/solution.py
@@ -13,8 +13,9 @@
 HALF = 1024
 WIDE = 2048
 LAYERS = 8
-STRIP = 1024
-EARLY = 40
+STRIP = 512
+FIRST = 24
+DIRECT = 48
 COPIES = 32
 
 
@@ -55,7 +56,7 @@
 def kernel(
     e_hbm, p_hbm, seabed_hbm, vol_hbm,
     new_e_out, new_p_out, lap_ref,
-    raw, one, new, seabed, vol, depth, column,
+    raw, one, new, seabed, vol, depth, column, north, east, coef,
     side_x, side_send, side_recv, side_in, relay, relay_two,
     rows_out, rows_in, ring_rows, new_rows_out, new_rows_in, cols_out, cols_in,
     local_sem, send_sem, recv_sem,
@@ -122,29 +123,62 @@
         return copy
 
 
-    raw_copies = []
+    row_halos, side_halos = [], []
+    for dx, src, dst in ((1, pl.ds(64, 8), pl.ds(0, 8)), (-1, pl.ds(8, 8), pl.ds(72, 8))):
+        row_halos.append(send(raw.at[:, src, inner], raw.at[:, dst, inner], device(dx, 0)))
     for d, db in ((0, 1), (1, -1)):
-        raw_copies.append(send(side_send.at[d], side_recv.at[d], device(0, db)))
+        side_halos.append(send(side_send.at[d], side_recv.at[d], device(0, db)))
         for dx, src, dst in ((1, pl.ds(56, 8), pl.ds(0, 8)), (-1, pl.ds(0, 8), pl.ds(72, 8))):
-            raw_copies.append(send(side_x.at[d, src], side_in.at[d, dst], device(dx, db)))
-    for dx, src, dst in ((1, pl.ds(64, 8), pl.ds(0, 8)), (-1, pl.ds(8, 8), pl.ds(72, 8))):
-        raw_copies.append(send(raw.at[:, src, inner], raw.at[:, dst, inner], device(dx, 0)))
-
-    rest = pl.ds(EARLY, ROWS - EARLY)
-    rest_in = pl.ds(8 + EARLY, ROWS - EARLY)
-    bound_early = send(
-        vol_hbm.at[edge, pl.ds(0, EARLY)], vol.at[theirs, pl.ds(8, EARLY), tile], partner
+            row_halos.append(send(side_x.at[d, src], side_in.at[d, dst], device(dx, db)))
+
+    last = pl.ds(DIRECT, ROWS - DIRECT)
+    last_in = pl.ds(8 + DIRECT, ROWS - DIRECT)
+    hops = [
+        message(vol_hbm.at[7, last], relay, opposite),
+        message(relay, relay_two, partner),
+        message(relay_two, vol.at[0, last_in, tile], opposite),
+    ]
+
+    @pl.when(gz == 0)
+    def _():
+        hops[0].start()
+
+    loads[2].wait()
+    loads[3].wait()
+    for d, row in ((0, 63), (1, 0)):
+
+        @pl.loop(0, LAYERS)
+        def _(k):
+            for t in range(16):
+                rows_out[d, k, pl.ds(t, 1), :] = vol[
+                    k + 1, pl.ds(row + 8, 1), pl.ds(128 + 128 * t, 128)
+                ]
+
+        for t in range(16):
+            bed = seabed[pl.ds(row, 1), pl.ds(128 + 128 * t, 128)]
+            rows_out[d, LAYERS, pl.ds(t, 1), :] = bed.astype(jnp.float32) * DEPTH_UNIT
+    row_copies = []
+    for d, dx in ((0, 1), (1, -1)):
+        row_copies.append(send(rows_out.at[d], rows_in.at[d], device(dx, 0)))
+        row_copies.append(send(rows_out.at[d, edge], ring_rows.at[d], device(dx, side)))
+
+    bound_first = send(
+        vol_hbm.at[edge, pl.ds(0, FIRST)], vol.at[theirs, pl.ds(8, FIRST), tile], partner
     )
-    bound_late = message(vol_hbm.at[0, rest], vol.at[9, rest_in, tile], partner)
-    hops = [
-        message(vol_hbm.at[7, rest], relay, opposite),
-        message(relay, relay_two, partner),
-        message(relay_two, vol.at[0, rest_in, tile], opposite),
-    ]
+    bound_next = message(
+        vol_hbm.at[7, pl.ds(FIRST, DIRECT - FIRST)],
+        vol.at[0, pl.ds(8 + FIRST, DIRECT - FIRST), tile],
+        partner,
+    )
+    bound_late = message(
+        vol_hbm.at[0, pl.ds(FIRST, ROWS - FIRST)],
+        vol.at[9, pl.ds(8 + FIRST, ROWS - FIRST), tile],
+        partner,
+    )
 
     @pl.when(gz == 0)
     def _():
-        hops[0].start()
+        bound_next.start()
 
     side_copies = []
     for by, src, dst in (
@@ -155,34 +189,12 @@
         side_copies.append(send(vol_hbm.at[:, :, src], vol.at[pl.ds(1, LAYERS), mid, dst], to))
         side_copies.append(send(seabed_hbm.at[:, src], seabed.at[:, dst], to))
 
-    loads[2].wait()
-    loads[3].wait()
-    for d, row in ((0, 63), (1, 0)):
-
-        @pl.loop(0, LAYERS)
-        def _(k):
-            for t in range(16):
-                rows_out[d, k, pl.ds(t, 1), :] = vol[
-                    k + 1, pl.ds(row + 8, 1), pl.ds(128 + 128 * t, 128)
-                ]
-
-        for t in range(16):
-            bed = seabed[pl.ds(row, 1), pl.ds(128 + 128 * t, 128)]
-            rows_out[d, LAYERS, pl.ds(t, 1), :] = bed.astype(jnp.float32) * DEPTH_UNIT
-    row_copies = []
-    for d, dx in ((0, 1), (1, -1)):
-        row_copies.append(send(rows_out.at[d], rows_in.at[d], device(dx, 0)))
-        row_copies.append(send(rows_out.at[d, edge], ring_rows.at[d], device(dx, side)))
-
-    for copy in raw_copies:
-        copy.wait_recv()
-    for d in (0, 1):
-        back = jnp.transpose(side_recv[d])
-        side_in[d, mid, pl.ds(0, 16)] = back[:ROWS]
-        block_in = side_in[d]
-        at = pl.ds(0, 128) if d == 0 else pl.ds(HALF + 128, 128)
-        raw[0, :, at] = pltpu.roll(block_in, 120, axis=1) if d == 0 else block_in
-        raw[1, :, at] = pltpu.roll(block_in, 112 if d == 0 else 120, axis=1)
+    def place_sides(rows):
+        for d in (0, 1):
+            block_in = side_in[d, rows, :]
+            at = pl.ds(0, 128) if d == 0 else pl.ds(HALF + 128, 128)
+            raw[0, rows, at] = pltpu.roll(block_in, 120, axis=1) if d == 0 else block_in
+            raw[1, rows, at] = pltpu.roll(block_in, 112 if d == 0 else 120, axis=1)
 
     def tiles(ref, lead, r):
         def rows(i):
@@ -190,32 +202,56 @@
 
         return rows(jnp.maximum(r - 1, 0)), rows(r), rows(jnp.minimum(r + 1, 9))
 
-    @pl.loop(0, 10)
-    def _(r):
-        height, poten = tiles(raw, (0,), r), tiles(raw, (1,), r)
-        rate_height, rate_poten = section(height, poten)
-        at = pl.ds(pl.multiple_of(8 * r, 8), 8)
-        one[0, at, :] = height[1] + TIME_STEP * rate_height
-        one[1, at, :] = poten[1] + TIME_STEP * rate_poten
+    def first_section(begin, end):
+        @pl.loop(begin, end, unroll=True)
+        def _(r):
+            height, poten = tiles(raw, (0,), r), tiles(raw, (1,), r)
+            rate_height, rate_poten = section(height, poten)
+            at = pl.ds(pl.multiple_of(8 * r, 8), 8)
+            one[0, at, :] = height[1] + TIME_STEP * rate_height
+            one[1, at, :] = poten[1] + TIME_STEP * rate_poten
+
+    def second_section(begin, end):
+        @pl.loop(begin, end, unroll=True)
+        def _(r):
+            height, poten = tiles(one, (0,), r), tiles(one, (1,), r)
+            rates = section(height, poten)
+            at = pl.ds(pl.multiple_of(8 * r, 8), 8)
+            for f in (0, 1):
+                first = (height, poten)[f][1]
+                new[0, f, at, :] = 0.5 * (raw[f, at, :] + first + TIME_STEP * rates[f])
+
+    def field(f, begin, count):
+        rows = pl.ds(begin, count)
+        return message(new.at[0, f, rows, inner], new.at[1, f, rows, inner], partner)
+
+    height_copies = [field(0, 24, 32), field(0, 8, 16), field(0, 56, 16)]
+    poten_copies = [field(1, 8, 32), field(1, 40, 32)]
+
+    for copy in side_halos:
+        copy.wait_recv()
+    for d in (0, 1):
+        side_in[d, mid, pl.ds(0, 16)] = jnp.transpose(side_recv[d])[:ROWS]
+    place_sides(mid)
+    first_section(2, 8)
 
     @pl.when(gz == 1)
     def _():
         hops[0].wait_recv()
         hops[1].start()
 
-    @pl.loop(0, 10)
-    def _(r):
-        height, poten = tiles(one, (0,), r), tiles(one, (1,), r)
-        rates = section(height, poten)
-        at = pl.ds(pl.multiple_of(8 * r, 8), 8)
-        for f in (0, 1):
-            first = (height, poten)[f][1]
-            new[0, f, at, :] = 0.5 * (raw[f, at, :] + first + TIME_STEP * rates[f])
-
-    field_copies = [
-        message(new.at[0, f, mid, inner], new.at[1, f, mid, inner], partner) for f in (0, 1)
-    ]
-    field_copies[0].start()
+    second_section(3, 7)
+    height_copies[0].start()
+    for copy in row_halos:
+        copy.wait_recv()
+    place_sides(pl.ds(0, 8))
+    place_sides(pl.ds(72, 8))
+    first_section(0, 2)
+    first_section(8, 10)
+    second_section(0, 3)
+    height_copies[1].start()
+    second_section(7, 10)
+    height_copies[2].start()
 
     for f in (0, 1):
         for d, row in ((0, 7), (1, 72)):
@@ -266,89 +302,137 @@
             at = pl.ds(128 + 128 * t, 128)
             depth[pl.ds(row, 1), at] = rows_in[d, LAYERS, pl.ds(t, 1), :]
 
-    def prepare(h, do_column, do_top):
-        base = pl.multiple_of(HALF * (gz if h == 0 else 1 - gz), 128)
-        span = pl.ds(base, HALF + 256)
-
-        @pl.loop(0, 10)
+    def start_of(h):
+        return HALF * (gz if h == 0 else 1 - gz)
+
+    def around(ref, lead, row, lane):
+        def rows(at, lanes):
+            return ref[lead + (pl.ds(at, 8), lanes)]
+
+        wide = rows(row, pl.ds(lane, HALF + 256))
+        here = wide[:, 128 : 128 + HALF]
+        centre = pl.ds(pl.multiple_of(lane + 128, 128), HALF)
+        before, after = rows(row - 8, centre), rows(row + 8, centre)
+        up, down = row_shift(before, here, after, 1), row_shift(before, here, after, -1)
+        right = lane_shift(wide, 1)[:, 128 : 128 + HALF]
+        left = lane_shift(wide, -1)[:, 128 : 128 + HALF]
+        return here, up - down, right - left, (up + down) + (right + left)
+
+    def difference(layer, r, lane, flat):
+        row = pl.multiple_of(8 * r, 8)
+        here, by_row, by_lane, total = around(vol, (layer,), pl.multiple_of(row + 8, 8), lane)
+        at = (pl.ds(row, 8), pl.ds(lane, HALF))
+        north[(layer,) + at] = by_row
+        east[(layer,) + at] = by_lane
+        if flat:
+            lap_ref[(layer - 1,) + at] = total - 4.0 * here
+
+    def differences(layer, h, first_tile, last_tile, flat):
+        lane = pl.multiple_of(start_of(h), 128)
+
+        @pl.loop(first_tile, last_tile, unroll=True)
+        def _(r):
+            difference(layer, r, lane, flat)
+
+    def coefficients(h):
+        lane = pl.multiple_of(start_of(h), 128)
+        span = pl.ds(lane, HALF + 256)
+
+        @pl.loop(0, 10, unroll=2)
         def _(r):
             at = pl.ds(pl.multiple_of(8 * r, 8), 8)
-            if do_column:
-                column[h, at, :] = depth[at, span] + new[h, 0, at, :]
-
-                @pl.when(gz == 0)
-                def _():
-                    vol[0, at, span] = vol[1, at, span]
-
-            if do_top:
-
-                @pl.when(gz == 1)
-                def _():
-                    vol[9, at, span] = 2.0 * new[h, 1, at, :] - vol[8, at, span]
-
-    def laplace(h, start, count, first_tile, last_tile):
-        base = HALF * (gz if h == 0 else 1 - gz)
-        sigma = ((8 * gz + start).astype(jnp.float32) + 0.5) * 0.0625
-
-        @pl.loop(first_tile, last_tile)
+            column[h, at, :] = depth[at, span] + new[h, 0, at, :]
+
+        @pl.loop(0, 8, unroll=4)
         def _(r):
-            row = pl.multiple_of(8 * r + 8, 8)
-
-            @pl.loop(0, HALF // STRIP)
+            row = pl.multiple_of(8 * r, 8)
+            inside = pl.multiple_of(row + 8, 8)
+            here, column_north, column_east, _ = around(column, (h,), inside, 0)
+            _, depth_north, depth_east, _ = around(depth, (), inside, lane)
+            inverse = 1.0 / here
+            scale = 4.0 * inverse
+            at = (pl.ds(row, 8), pl.ds(lane, HALF))
+            coef[(0,) + at] = depth_north * scale
+            coef[(1,) + at] = column_north * scale
+            coef[(2,) + at] = depth_east * scale
+            coef[(3,) + at] = column_east * scale
+            coef[(4,) + at] = 64.0 * inverse * inverse
+
+    def top(h, begin, end):
+        span = pl.ds(pl.multiple_of(start_of(h), 128), HALF + 256)
+
+        @pl.loop(begin, end)
+        def _(r):
+            at = pl.ds(pl.multiple_of(8 * r, 8), 8)
+            vol[9, at, span] = 2.0 * new[h, 1, at, :] - vol[8, at, span]
+
+    def combine(h, start, count, first_tile, last_tile):
+        base = start_of(h)
+        sigma = (jnp.asarray(8 * gz + start, jnp.int32).astype(jnp.float32) + 0.5) * 0.0625
+        lowest = jnp.where(start + gz == 0, 1, start)
+
+        strip = HALF if count == 1 else STRIP
+
+        @pl.loop(first_tile, last_tile, unroll=count == 1)
+        def _(r):
+            rows = pl.ds(pl.multiple_of(8 * r, 8), 8)
+            inside = pl.ds(pl.multiple_of(8 * r + 8, 8), 8)
+
+            @pl.loop(0, HALF // strip)
             def _(s):
-                lane = pl.multiple_of(s * STRIP, 128)
-                full = pl.multiple_of(base + lane, 128)
-
-                def around(ref, lead, lane):
-                    def rows(at, lanes):
-                        return ref[lead + (pl.ds(at, 8), lanes)]
-
-                    wide = rows(row, pl.ds(lane, STRIP + 256))
-                    here = wide[:, 128 : 128 + STRIP]
-                    centre = pl.ds(pl.multiple_of(lane + 128, 128), STRIP)
-                    before, after = rows(row - 8, centre), rows(row + 8, centre)
-                    up = row_shift(before, here, after, 1)
-                    down = row_shift(before, here, after, -1)
-                    right = lane_shift(wide, 1)[:, 128 : 128 + STRIP]
-                    left = lane_shift(wide, -1)[:, 128 : 128 + STRIP]
-                    return here, up - down, right - left, (up + down) + (right + left)
-
-                here, column_north, column_east, _ = around(column, (h,), lane)
-                _, depth_north, depth_east, _ = around(depth, (), full)
-                inverse = 1.0 / here
-                scale = 4.0 * inverse
-                step_north = column_north * scale
-                step_east = column_east * scale
-                slope_north = depth_north * scale - sigma * step_north
-                slope_east = depth_east * scale - sigma * step_east
+                lane = base + s * strip
+                at = (rows, pl.ds(pl.multiple_of(lane, 128), strip))
+                centre = (inside, pl.ds(pl.multiple_of(lane + 128, 128), strip))
+
+                def load(layer):
+                    return (
+                        vol[(layer,) + centre], north[(layer,) + at], east[(layer,) + at]
+                    )
+
+                step_north, step_east = coef[(1,) + at], coef[(3,) + at]
+                slope_north = coef[(0,) + at] - sigma * step_north
+                slope_east = coef[(2,) + at] - sigma * step_east
                 step_north = step_north * 0.0625
                 step_east = step_east * 0.0625
-                bottom = 64.0 * inverse * inverse
-                below = around(vol, (start,), full)
-                middle = around(vol, (start + 1,), full)
+                bottom = coef[(4,) + at]
+                below, middle = load(lowest), load(start + 1)
                 for k in range(count):
-                    above = around(vol, (start + k + 2,), full)
+                    above = load(start + k + 2)
                     weight = slope_north * slope_north + slope_east * slope_east + bottom
-                    four = 4.0 * middle[0]
-                    vertical = 4.0 * (above[0] + below[0]) - 2.0 * four
-                    lap_ref[start + k, pl.ds(row - 8, 8), pl.ds(full, STRIP)] = (
-                        (middle[3] - four)
+                    vertical = 4.0 * (above[0] + below[0]) - 8.0 * middle[0]
+                    lap_ref[(start + k,) + at] = (
+                        lap_ref[(start + k,) + at]
                         + slope_north * (above[1] - below[1])
                         + slope_east * (above[2] - below[2])
                         + weight * vertical
                     )
-                    slope_north = slope_north - step_north
-                    slope_east = slope_east - step_east
+                    if k < count - 1:
+                        slope_north = slope_north - step_north
+                        slope_east = slope_east - step_east
                     below, middle = middle, above
 
-    prepare(0, True, True)
-    laplace(0, gz, LAYERS - 1, 0, 8)
+    @pl.loop(0, 8)
+    def _(r):
+        @pl.loop(0, 2)
+        def _(s):
+            for layer in range(1, LAYERS + 1):
+                difference(layer, r, pl.multiple_of(HALF * s, 128), True)
 
     @pl.when(gz == 0)
     def _():
-        field_copies[1].start()
+        for copy in poten_copies:
+            copy.start()
         hops[1].wait_recv()
         hops[2].start()
+
+    @pl.when(gz == 1)
+    def _():
+        bound_late.start()
+        top(0, 0, 10)
+        differences(9, 0, 0, 8, False)
+
+    coefficients(0)
+    combine(0, gz, LAYERS - 1, 0, 8)
 
     for copy in ring_copies:
         copy.wait_recv()
@@ -371,40 +455,58 @@
         new[1, f, mid, pl.ds(far, 128)] = pick(back, 126 - f, 125 - f)
         new[1, f, mid, pl.ds(close, 128)] = new[0, f, mid, pl.ds(inside, 128)]
 
-    bound_early.wait_recv()
-    split = EARLY // 8 - 1
-    laplace(0, edge, 1, 0, split)
+    bound_first.wait_recv()
 
     @pl.when(gz == 1)
     def _():
-        field_copies[0].wait_send()
-        bound_late.start()
-
-    field_copies[0].wait_recv()
-    prepare(1, True, False)
+        bound_next.wait_recv()
+
+    def other_half():
+        for copy in height_copies:
+            copy.wait_recv()
+        coefficients(1)
 
     @pl.when(gz == 0)
     def _():
-        laplace(1, 0, LAYERS - 1, 0, 8)
-        laplace(1, LAYERS - 1, 1, 0, split)
+        split = FIRST // 8 - 1
+        for h in (0, 1):
+            differences(9, h, 0, split, False)
+        combine(0, LAYERS - 1, 1, 0, split)
+        other_half()
+        combine(1, 0, LAYERS - 1, 0, 8)
+        combine(1, LAYERS - 1, 1, 0, split)
         bound_late.wait_recv()
         for h in (0, 1):
-            laplace(h, LAYERS - 1, 1, split, 8)
+            differences(9, h, split, 8, False)
+            combine(h, LAYERS - 1, 1, split, 8)
 
     @pl.when(gz == 1)
     def _():
-        laplace(1, 1, LAYERS - 2, 0, 8)
-        laplace(1, 0, 1, 0, split)
+        split = DIRECT // 8 - 1
+        for h in (0, 1):
+            differences(0, h, 0, split, False)
+        combine(0, 0, 1, 0, split)
+        other_half()
+        combine(1, 1, LAYERS - 2, 0, 8)
+        combine(1, 0, 1, 0, split)
         hops[2].wait_recv()
         for h in (0, 1):
-            laplace(h, 0, 1, split, 8)
-        field_copies[1].wait_recv()
-        prepare(1, False, True)
-        laplace(1, LAYERS - 1, 1, 0, 8)
+            differences(0, h, split, 8, False)
+            combine(h, 0, 1, split, 8)
+        for copy, (begin, end), (first, last) in zip(
+            poten_copies, ((0, 5), (5, 10)), ((0, 3), (3, 8))
+        ):
+            copy.wait_recv()
+            top(1, begin, end)
+            differences(9, 1, first, last, False)
+            combine(1, LAYERS - 1, 1, first, last)
+
+    for copy in height_copies:
+        copy.wait_send()
 
     @pl.when(gz == 0)
     def _():
-        for copy in (*field_copies, hops[0], hops[2]):
+        for copy in (*poten_copies, bound_next, hops[0], hops[2]):
             copy.wait_send()
 
     @pl.when(gz == 1)
@@ -417,10 +519,9 @@
 
 
 def write(e_ref, p_ref, lap_ref, e_out, p_out, lap_out, sem):
-    copies = [
-        pltpu.make_async_copy(src, dst, sem.at[i])
-        for i, (src, dst) in enumerate(((lap_ref, lap_out), (e_ref, e_out), (p_ref, p_out)))
-    ]
+    pairs = [(lap_ref.at[k], lap_out.at[k]) for k in range(LAYERS)]
+    pairs += [(e_ref, e_out), (p_ref, p_out)]
+    copies = [pltpu.make_async_copy(*pair, sem.at[i]) for i, pair in enumerate(pairs)]
     for copy in copies:
         copy.start()
     for copy in copies:
@@ -453,12 +554,15 @@
             pltpu.VMEM((LAYERS + 2, ROWS + 16, WIDE + 256), f32),
             pltpu.VMEM((ROWS + 16, WIDE + 256), f32),
             pltpu.VMEM((2, ROWS + 16, HALF + 256), f32),
+            pltpu.VMEM((LAYERS + 2, ROWS, WIDE), f32),
+            pltpu.VMEM((LAYERS + 2, ROWS, WIDE), f32),
+            pltpu.VMEM((5, ROWS, WIDE), f32),
             pltpu.VMEM((2, ROWS, 128), f32),
             pltpu.VMEM((2, 16, 128), f32),
             pltpu.VMEM((2, 16, 128), f32),
             pltpu.VMEM((2, ROWS + 16, 128), f32),
-            pltpu.VMEM((ROWS - EARLY, WIDE), f32),
-            pltpu.VMEM((ROWS - EARLY, WIDE), f32),
+            pltpu.VMEM((ROWS - DIRECT, WIDE), f32),
+            pltpu.VMEM((ROWS - DIRECT, WIDE), f32),
             pltpu.VMEM((2, LAYERS + 1, 16, 128), f32),
             pltpu.VMEM((2, LAYERS + 1, 16, 128), f32),
             pltpu.VMEM((2, 16, 128), f32),
@@ -471,7 +575,7 @@
             pltpu.SemaphoreType.DMA((COPIES,)),
         ],
         compiler_params=pltpu.CompilerParams(
-            collective_id=0, has_side_effects=True, vmem_limit_bytes=40 << 20
+            collective_id=0, has_side_effects=True, vmem_limit_bytes=48 << 20
         ),
         name="wave_step",
     )(*operands)
@@ -480,7 +584,7 @@
         out_shape=tuple(jax.ShapeDtypeStruct(x.shape, f32) for x in results),
         in_specs=[vmem] * 3,
         out_specs=(hbm,) * 3,
-        scratch_shapes=[pltpu.SemaphoreType.DMA((3,))],
+        scratch_shapes=[pltpu.SemaphoreType.DMA((LAYERS + 2,))],
         compiler_params=pltpu.CompilerParams(vmem_limit_bytes=4 << 20),
         name="write_results",
     )(*(pltpu.with_memory_space_constraint(x, pltpu.VMEM) for x in results))

time: 37.4 us -> 33.3 us (0.89); the launches traced: 36.7 us -> 33.2 us
  Pallas kernels: 36 us -> 32.5 us
    pallas_call x1, Pallas kernels: 33.9 us -> 30.3 us  [shards(): pl.pallas_call(kernel, out_shape=held, in_specs=[hbm] * 4, out_specs=(vme...]
where the time goes in v4:
time: 33.3 us; the launch traced here: 33.2 us
  Pallas kernels  32.5 us (98%)
  between operations  0.64 us (2%)
    pallas_call x1, Pallas kernels, shards(): pl.pallas_call(kernel, out_shape=held, in_specs=[hbm] * 4, out_specs=(vme...  30.3 us
    pallas_call x1, Pallas kernels, shards(): pl.pallas_call(write, out_shape=tuple((jax.ShapeDtypeStruct(x.shape, f32)...  2.25 us

profile of v4, /device:TPU:8, one launch (start us, length us, event | category | flops | bytes accessed | tf_op | source)
XLA Modules:
  0.0 33.2 jit_solution(3770328822558637256)
XLA Ops:
  0.6 30.3 %wave_step.1 = (f32[64,1024]{1,0:T(8,128)S(1)}, f32[64,1024]{1,0:T(8,128)S(1)}, f32[8,64,2048]{2,1,0:T(8,128)S(1)}) custom-call(f32[64,1024]{1,0:T(8,128)} %e_hbm.1, f32[64,1024]{1,0:T(8,128)} %p_hbm.1, s32[64,2048]{1,0:T(8,128)} %seabed_hbm.1, f32[8,64,2048]{2,1,0:T(8,128)} %vol_hbm.1), custom_call_target="tpu_custom_call" | custom-call | tf_op jit(solution)/shard_map/wave_step/pallas_call | solution.py:544
  30.9 2.2 %write_results.1 = (f32[64,1024]{1,0:T(8,128)}, f32[64,1024]{1,0:T(8,128)}, f32[8,64,2048]{2,1,0:T(8,128)}) custom-call(f32[64,1024]{1,0:T(8,128)S(1)} %get-tuple-element.6.e_ref, f32[64,1024]{1,0:T(8,128)S(1)} %get-tuple-element.7.p_ref, f32[8,64,2048]{2,1,0:T(8,128)S(1)} %get-tuple-element.8.lap_ref), custom_call_target="tpu_custom_call" | custom-call | tf_op jit(solution)/shard_map/write_results/pallas_call | solution.py:582

commit v5 on v4

--- a/solution.py
+++ b/solution.py
@@ -14,7 +14,8 @@
 WIDE = 2048
 LAYERS = 8
 STRIP = 512
-FIRST = 24
+LATE = 48
+FIRST = 32
 DIRECT = 48
 COPIES = 32
 
@@ -170,11 +171,14 @@
         vol.at[0, pl.ds(8 + FIRST, DIRECT - FIRST), tile],
         partner,
     )
-    bound_late = message(
-        vol_hbm.at[0, pl.ds(FIRST, ROWS - FIRST)],
-        vol.at[9, pl.ds(8 + FIRST, ROWS - FIRST), tile],
-        partner,
-    )
+    bound_late = [
+        message(
+            vol_hbm.at[0, pl.ds(begin, end - begin)],
+            vol.at[9, pl.ds(8 + begin, end - begin), tile],
+            partner,
+        )
+        for begin, end in ((FIRST, LATE), (LATE, ROWS))
+    ]
 
     @pl.when(gz == 0)
     def _():
@@ -288,19 +292,6 @@
     def _(r):
         at = pl.multiple_of(8 * r, 8)
         depth[pl.ds(at + 8, 8), :] = seabed[pl.ds(at, 8), :].astype(jnp.float32) * DEPTH_UNIT
-
-    for copy in row_copies:
-        copy.wait_recv()
-    for d, row in ((0, 7), (1, 72)):
-
-        @pl.loop(0, LAYERS)
-        def _(k):
-            for t in range(16):
-                vol[k + 1, pl.ds(row, 1), pl.ds(128 + 128 * t, 128)] = rows_in[d, k, pl.ds(t, 1), :]
-
-        for t in range(16):
-            at = pl.ds(128 + 128 * t, 128)
-            depth[pl.ds(row, 1), at] = rows_in[d, LAYERS, pl.ds(t, 1), :]
 
     def start_of(h):
         return HALF * (gz if h == 0 else 1 - gz)
@@ -411,12 +402,15 @@
                         slope_east = slope_east - step_east
                     below, middle = middle, above
 
-    @pl.loop(0, 8)
-    def _(r):
-        @pl.loop(0, 2)
-        def _(s):
-            for layer in range(1, LAYERS + 1):
-                difference(layer, r, pl.multiple_of(HALF * s, 128), True)
+    def all_layers(begin, end, step):
+        @pl.loop(begin, end, step=step)
+        def _(r):
+            @pl.loop(0, 2)
+            def _(s):
+                for layer in range(1, LAYERS + 1):
+                    difference(layer, r, pl.multiple_of(HALF * s, 128), True)
+
+    all_layers(1, 7, 1)
 
     @pl.when(gz == 0)
     def _():
@@ -427,7 +421,26 @@
 
     @pl.when(gz == 1)
     def _():
-        bound_late.start()
+        for copy in bound_late:
+            copy.start()
+
+    for copy in row_copies:
+        copy.wait_recv()
+    for d, row in ((0, 7), (1, 72)):
+
+        @pl.loop(0, LAYERS)
+        def _(k):
+            for t in range(16):
+                vol[k + 1, pl.ds(row, 1), pl.ds(128 + 128 * t, 128)] = rows_in[d, k, pl.ds(t, 1), :]
+
+        for t in range(16):
+            at = pl.ds(128 + 128 * t, 128)
+            depth[pl.ds(row, 1), at] = rows_in[d, LAYERS, pl.ds(t, 1), :]
+
+    all_layers(0, 8, 7)
+
+    @pl.when(gz == 1)
+    def _():
         top(0, 0, 10)
         differences(9, 0, 0, 8, False)
 
@@ -475,10 +488,11 @@
         other_half()
         combine(1, 0, LAYERS - 1, 0, 8)
         combine(1, LAYERS - 1, 1, 0, split)
-        bound_late.wait_recv()
-        for h in (0, 1):
-            differences(9, h, split, 8, False)
-            combine(h, LAYERS - 1, 1, split, 8)
+        for copy, first, last in zip(bound_late, (split, LATE // 8 - 1), (LATE // 8 - 1, 8)):
+            copy.wait_recv()
+            for h in (0, 1):
+                differences(9, h, first, last, False)
+                combine(h, LAYERS - 1, 1, first, last)
 
     @pl.when(gz == 1)
     def _():
@@ -511,7 +525,7 @@
 
     @pl.when(gz == 1)
     def _():
-        for copy in (hops[1], bound_late):
+        for copy in (hops[1], *bound_late):
             copy.wait_send()
 
     for copy in started:

time: 33.3 us -> 33.3 us (level)
  no operation moved by 1% of the time
where the time goes in v5:
time: 33.3 us; the launch traced here: 33.2 us
  Pallas kernels  32.5 us (98%)
  between operations  0.64 us (2%)
    pallas_call x1, Pallas kernels, shards(): pl.pallas_call(kernel, out_shape=held, in_specs=[hbm] * 4, out_specs=(vme...  30.3 us
    pallas_call x1, Pallas kernels, shards(): pl.pallas_call(write, out_shape=tuple((jax.ShapeDtypeStruct(x.shape, f32)...  2.25 us

profile of v5, /device:TPU:8, one launch (start us, length us, event | category | flops | bytes accessed | tf_op | source)
XLA Modules:
  0.0 33.2 jit_solution(5661427537627942237)
XLA Ops:
  0.6 30.3 %wave_step.1 = (f32[64,1024]{1,0:T(8,128)S(1)}, f32[64,1024]{1,0:T(8,128)S(1)}, f32[8,64,2048]{2,1,0:T(8,128)S(1)}) custom-call(f32[64,1024]{1,0:T(8,128)} %e_hbm.1, f32[64,1024]{1,0:T(8,128)} %p_hbm.1, s32[64,2048]{1,0:T(8,128)} %seabed_hbm.1, f32[8,64,2048]{2,1,0:T(8,128)} %vol_hbm.1), custom_call_target="tpu_custom_call" | custom-call | tf_op jit(solution)/shard_map/wave_step/pallas_call | solution.py:558
  30.9 2.2 %write_results.1 = (f32[64,1024]{1,0:T(8,128)}, f32[64,1024]{1,0:T(8,128)}, f32[8,64,2048]{2,1,0:T(8,128)}) custom-call(f32[64,1024]{1,0:T(8,128)S(1)} %get-tuple-element.6.e_ref, f32[64,1024]{1,0:T(8,128)S(1)} %get-tuple-element.7.p_ref, f32[8,64,2048]{2,1,0:T(8,128)S(1)} %get-tuple-element.8.lap_ref), custom_call_target="tpu_custom_call" | custom-call | tf_op jit(solution)/shard_map/write_results/pallas_call | solution.py:596
